TPU v7x, 32 devices: a whole 2x2x4 slice. The times are simulated.
32 devices in a mesh: dp: 8 (over y, x, core), mp: 4 (over z).
Axes of the slice: x: 2, y: 2, z: 4, core: 2. Of those that a mesh axis runs over, the one named last changes fastest.
Arguments:
- inputs: bfloat16 [16, 1024, 1280], P('dp', 'mp'), may hold values from -6 to 6
- cotangent: bfloat16 [16, 1024, 1280], P('dp', 'mp'), may hold values from -6 to 6
- gene_counts: int32 [16], P('dp'), may hold values from 200 to 1023, as said below
- step_count: int32 [1], replicated, may hold values from 2 to 20
- norm_params: float32 [4, 1280], P(None, ('dp', 'mp')), may hold values from -0.3 to 1.4, as said below
- norm_first: float32 [4, 1280], P(None, ('dp', 'mp')), may hold values from -80 to 80
- norm_second: float32 [4, 1280], P(None, ('dp', 'mp')), may hold values from 425.984 to 6881.28
- attend_weight: float32 [3, 1280, 1280], P(None, 'dp', 'mp'), may hold values from -0.15625 to 0.15625
- attend_first: float32 [3, 1280, 1280], P(None, 'dp', 'mp'), may hold values from -80 to 80
- attend_second: float32 [3, 1280, 1280], P(None, 'dp', 'mp'), may hold values from 425.984 to 6881.28
- output_weight: float32 [1280, 1280], P('mp', 'dp'), may hold values from -4 to 4
- output_first: float32 [1280, 1280], P('mp', 'dp'), may hold values from -4 to 4
- output_second: float32 [1280, 1280], P('mp', 'dp'), may hold values from 0.8 to 13.44
- expand_weight: float32 [1280, 5120], P('dp', 'mp'), may hold values from -0.15625 to 0.15625
- expand_first: float32 [1280, 5120], P('dp', 'mp'), may hold values from -32 to 32
- expand_second: float32 [1280, 5120], P('dp', 'mp'), may hold values from 68.8128 to 1097.728
- reduce_weight: float32 [5120, 1280], P('mp', 'dp'), may hold values from -0.078125 to 0.078125
- reduce_first: float32 [5120, 1280], P('mp', 'dp'), may hold values from -48 to 48
- reduce_second: float32 [5120, 1280], P('mp', 'dp'), may hold values from 155.648 to 2457.6
Outputs:
- outputs: float32 [16, 1024, 1280], P('dp', 'mp')
- input_grad: float32 [16, 1024, 1280], P('dp', 'mp')
- norm_master: float32 [4, 1280], P(None, ('dp', 'mp'))
- norm_momentum: float32 [4, 1280], P(None, ('dp', 'mp'))
- norm_variance: float32 [2, 1280], P(None, ('dp', 'mp'))
- feed_variance: float32 [2, 1280], P(None, ('dp', 'mp'))
- attend_master: float32 [3, 1280, 1280], P(None, 'dp', 'mp')
- attend_momentum: float32 [3, 1280, 1280], P(None, 'dp', 'mp')
- attend_variance: float32 [3, 1280, 1280], P(None, 'dp', 'mp')
- output_master: float32 [1280, 1280], P('mp', 'dp')
- output_momentum: float32 [1280, 1280], P('mp', 'dp')
- output_variance: float32 [1280, 1280], P('mp', 'dp')
- expand_master: float32 [1280, 5120], P('dp', 'mp')
- expand_momentum: float32 [1280, 5120], P('dp', 'mp')
- expand_variance: float32 [1280, 5120], P('dp', 'mp')
- reduce_master: float32 [5120, 1280], P('mp', 'dp')
- reduce_momentum: float32 [5120, 1280], P('mp', 'dp')
- reduce_variance: float32 [5120, 1280], P('mp', 'dp')
Inputs may be any that keep to these rules, and one draw needn't show every extreme that they name: `gene_counts`: genes of each cell; the cell holds that many tokens plus its CLS token, the rest of its 1024 slots are padding; the largest, 1023, occurs in every draw. `norm_params`: rows 0 and 2 are gains, rows 1 and 3 shifts.
All inputs are finite; a program needn't handle non-finite values.
Results may differ from a plain program's by a relative error of at most 0.012.
Values may be sent and summed in bfloat16 or wider, within the bound.
A program may use at most 256 MiB of HBM per device.

v0:
```python
import jax
import jax.numpy as jnp
from jax import lax
from jax.sharding import PartitionSpec as P

D = 1280
HEAD_DIM = 64
FF = 5120
SEQ = 1024


eps_norm = 1e-05
masked_score = -1e30
beta_one = 0.9
beta_two = 0.95
eps_adam = 1e-08
decay_rate = 0.1
norm_rate = 0.6


def exact_gelu(values):
    return jax.nn.gelu(values, approximate=False)


def contract_rows(left_side, right_side):
    return lax.dot_general(
        left_side, right_side, (((0,), (0,)), ((), ())), preferred_element_type=jnp.float32
    )


def times_transposed(left_side, right_side):
    return lax.dot_general(
        left_side, right_side, (((1,), (1,)), ((), ())), preferred_element_type=jnp.float32
    )


def normalize(token_rows, norm_gain, norm_shift):
    mean_row = jnp.mean(token_rows, axis=-1, keepdims=True)
    centred = token_rows - mean_row
    inv_std = lax.rsqrt(jnp.mean(centred * centred, axis=-1, keepdims=True) + eps_norm)
    scaled = centred * inv_std
    return (scaled * norm_gain + norm_shift, scaled, inv_std)


def normalize_back(grad_out, scaled, inv_std, norm_gain):
    grad_scaled = grad_out * norm_gain
    centre_part = jnp.mean(grad_scaled, axis=-1, keepdims=True)
    along_part = scaled * jnp.mean(grad_scaled * scaled, axis=-1, keepdims=True)
    grad_in = inv_std * (grad_scaled - centre_part - along_part)
    return (grad_in, jnp.sum(grad_out * scaled, axis=0), jnp.sum(grad_out, axis=0))


def gather_rows(values):
    return lax.all_gather(values, "mp", axis=0, tiled=True)


def reduce_rows(values):
    return lax.psum_scatter(values, "mp", scatter_dimension=0, tiled=True)


def gather_grads(values):
    return lax.all_gather(values, "mp", axis=0, tiled=True)


def reduce_grads(values):
    return lax.psum_scatter(values, "mp", scatter_dimension=0, tiled=True)


def head_scores(query_rows, key_heads, key_valid):
    raw_scores = jnp.einsum(
        "qhd,khd->hqk", query_rows, key_heads, preferred_element_type=jnp.float32
    ) * HEAD_DIM ** (-0.5)
    return jnp.where(key_valid[None, None, :], raw_scores, masked_score)


def attend(query_heads, key_heads, value_heads, key_valid):
    seq_len = query_heads.shape[0]
    block_rows = min(512, seq_len)
    contexts = []
    log_totals = []
    for row_start in range(0, seq_len, block_rows):
        scores = head_scores(query_heads[row_start : row_start + block_rows], key_heads, key_valid)
        row_max = jnp.max(scores, axis=-1, keepdims=True)
        exp_scores = jnp.exp(scores - row_max)
        row_total = jnp.sum(exp_scores, axis=-1, keepdims=True)
        probabilities = (exp_scores / row_total).astype(jnp.bfloat16)
        context = jnp.einsum(
            "hqk,khd->qhd", probabilities, value_heads, preferred_element_type=jnp.float32
        )
        contexts.append(context.astype(jnp.bfloat16))
        log_totals.append(row_max + jnp.log(row_total))
    return (jnp.concatenate(contexts, axis=0), jnp.concatenate(log_totals, axis=1))


def attend_back(query_heads, key_heads, value_heads, key_valid, log_totals, grad_context):
    seq_len = query_heads.shape[0]
    block_rows = min(512, seq_len)
    score_scale = HEAD_DIM ** (-0.5)
    grad_queries = []
    grad_keys = jnp.zeros(key_heads.shape, jnp.float32)
    grad_values = jnp.zeros(value_heads.shape, jnp.float32)
    for row_start in range(0, seq_len, block_rows):
        stop_row = row_start + block_rows
        query_rows = query_heads[row_start:stop_row]
        grad_block = grad_context[row_start:stop_row]
        scores = head_scores(query_rows, key_heads, key_valid)
        probabilities = jnp.exp(scores - log_totals[:, row_start:stop_row])
        grad_probs = jnp.einsum(
            "qhd,khd->hqk", grad_block, value_heads, preferred_element_type=jnp.float32
        )
        grad_values = grad_values + jnp.einsum(
            "hqk,qhd->khd",
            probabilities.astype(jnp.bfloat16),
            grad_block,
            preferred_element_type=jnp.float32,
        )
        inner_sum = jnp.sum(grad_probs * probabilities, axis=-1, keepdims=True)
        grad_scores = (probabilities * (grad_probs - inner_sum)).astype(jnp.bfloat16)
        grad_queries.append(
            jnp.einsum("hqk,khd->qhd", grad_scores, key_heads, preferred_element_type=jnp.float32)
            * score_scale
        )
        grad_keys = (
            grad_keys
            + jnp.einsum(
                "hqk,qhd->khd", grad_scores, query_rows, preferred_element_type=jnp.float32
            )
            * score_scale
        )
    return (jnp.concatenate(grad_queries, axis=0), grad_keys, grad_values)


def attention_forward(token_rows, norm_gain, norm_shift, attend_full, output_full, key_valid):
    normed, scaled, inv_std = normalize(token_rows, norm_gain, norm_shift)
    gathered = gather_rows(normed.astype(jnp.bfloat16))
    seq_len = gathered.shape[0]
    projected = jnp.einsum(
        "sd,tde->tse", gathered, attend_full, preferred_element_type=jnp.float32
    ).astype(jnp.bfloat16)
    head_shape = (seq_len, projected.shape[2] // HEAD_DIM, HEAD_DIM)
    query_heads = projected[0].reshape(head_shape)
    key_heads = projected[1].reshape(head_shape)
    value_heads = projected[2].reshape(head_shape)
    context, log_totals = attend(query_heads, key_heads, value_heads, key_valid)
    context_flat = context.reshape(seq_len, -1)
    branch = reduce_rows(jnp.dot(context_flat, output_full, preferred_element_type=jnp.float32))
    kept_state = (
        scaled,
        inv_std,
        gathered,
        query_heads,
        key_heads,
        value_heads,
        context_flat,
        log_totals,
    )
    return (token_rows + branch, kept_state)


def attention_back(grad_rows, kept_state, norm_gain, attend_full, output_full, key_valid):
    scaled, inv_std, gathered, query_heads, key_heads, value_heads, context_flat, log_totals = (
        kept_state
    )
    seq_len = gathered.shape[0]
    grad_full = gather_grads(grad_rows.astype(jnp.bfloat16))
    output_grad = contract_rows(context_flat, grad_full)
    grad_context = (
        times_transposed(grad_full, output_full).astype(jnp.bfloat16).reshape(query_heads.shape)
    )
    grad_query, grad_key, grad_value = attend_back(
        query_heads, key_heads, value_heads, key_valid, log_totals, grad_context
    )
    grad_proj = (
        jnp.stack([grad_query, grad_key, grad_value]).reshape(3, seq_len, -1).astype(jnp.bfloat16)
    )
    attend_grad = jnp.einsum("sd,tse->tde", gathered, grad_proj, preferred_element_type=jnp.float32)
    grad_normed = reduce_grads(
        jnp.einsum("tse,tde->sd", grad_proj, attend_full, preferred_element_type=jnp.float32)
    )
    grad_in, gain_grad, shift_grad = normalize_back(grad_normed, scaled, inv_std, norm_gain)
    return (grad_rows + grad_in, attend_grad, output_grad, gain_grad, shift_grad)


def feed_forward(token_rows, norm_gain, norm_shift, expand_full, reduce_full):
    normed, scaled, inv_std = normalize(token_rows, norm_gain, norm_shift)
    gathered = gather_rows(normed.astype(jnp.bfloat16))
    hidden = jnp.dot(gathered, expand_full, preferred_element_type=jnp.float32)
    active = exact_gelu(hidden).astype(jnp.bfloat16)
    branch = reduce_rows(jnp.dot(active, reduce_full, preferred_element_type=jnp.float32))
    return (token_rows + branch, (scaled, inv_std, gathered, hidden, active))


def feed_back(grad_rows, kept_state, norm_gain, expand_full, reduce_full):
    scaled, inv_std, gathered, hidden, active = kept_state
    grad_full = gather_grads(grad_rows.astype(jnp.bfloat16))
    reduce_grad = contract_rows(active, grad_full)
    grad_active = times_transposed(grad_full, reduce_full)
    grad_hidden = jax.vjp(exact_gelu, hidden)[1](grad_active)[0].astype(jnp.bfloat16)
    expand_grad = contract_rows(gathered, grad_hidden)
    grad_normed = reduce_grads(times_transposed(grad_hidden, expand_full))
    grad_in, gain_grad, shift_grad = normalize_back(grad_normed, scaled, inv_std, norm_gain)
    return (grad_rows + grad_in, expand_grad, reduce_grad, gain_grad, shift_grad)


def adam_step(weight, first_moment, second_moment, gradient, rate, decay, step_number):
    first_new = beta_one * first_moment + (1.0 - beta_one) * gradient
    second_new = beta_two * second_moment + (1.0 - beta_two) * gradient * gradient
    corr_one = 1.0 - jnp.power(beta_one, step_number)
    corr_two = 1.0 - jnp.power(beta_two, step_number)
    update = first_new / corr_one / (jnp.sqrt(second_new / corr_two) + eps_adam)
    return (weight - rate * (update + decay * weight), first_new, second_new)


def per_device(
    inputs,
    cotangent,
    gene_counts,
    step_count,
    norm_params,
    norm_first,
    norm_second,
    attend_weight,
    attend_first,
    attend_second,
    output_weight,
    output_first,
    output_second,
    expand_weight,
    expand_first,
    expand_second,
    reduce_weight,
    reduce_first,
    reduce_second,
):
    cell_count = inputs.shape[0]
    seq_len = inputs.shape[1] * lax.axis_size("mp")
    positions = jnp.arange(seq_len)
    norm_full = lax.all_gather(norm_params, ("dp", "mp"), axis=1, tiled=True)
    attend_full, output_full, expand_full, reduce_full = (
        lax.all_gather(attend_weight.astype(jnp.bfloat16), "dp", axis=1, tiled=True),
        lax.all_gather(output_weight.astype(jnp.bfloat16), "dp", axis=1, tiled=True),
        lax.all_gather(expand_weight.astype(jnp.bfloat16), "dp", axis=0, tiled=True),
        lax.all_gather(reduce_weight.astype(jnp.bfloat16), "dp", axis=1, tiled=True),
    )
    valid_masks = []
    attend_states = []
    middles = []
    for cell_index in range(cell_count):
        key_valid = positions < 1 + gene_counts[cell_index]
        middle, kept_state = attention_forward(
            inputs[cell_index].astype(jnp.float32),
            norm_full[0],
            norm_full[1],
            attend_full,
            output_full,
            key_valid,
        )
        valid_masks.append(key_valid)
        attend_states.append(kept_state)
        middles.append(middle)
    feed_states = []
    results = []
    for cell_index in range(cell_count):
        result, kept_state = feed_forward(
            middles[cell_index], norm_full[2], norm_full[3], expand_full, reduce_full
        )
        feed_states.append(kept_state)
        results.append(result)
    expand_sum = jnp.zeros(expand_full.shape, jnp.float32)
    reduce_sum = jnp.zeros(reduce_full.shape, jnp.float32)
    gain_two = jnp.zeros(norm_full.shape[1:], jnp.float32)
    shift_two = jnp.zeros(norm_full.shape[1:], jnp.float32)
    middle_grads = []
    for cell_index in range(cell_count):
        grad_middle, expand_grad, reduce_grad, gain_grad, shift_grad = feed_back(
            cotangent[cell_index].astype(jnp.float32),
            feed_states[cell_index],
            norm_full[2],
            expand_full,
            reduce_full,
        )
        expand_sum = expand_sum + expand_grad
        reduce_sum = reduce_sum + reduce_grad
        gain_two = gain_two + gain_grad
        shift_two = shift_two + shift_grad
        middle_grads.append(grad_middle)
    attend_sum = jnp.zeros(attend_full.shape, jnp.float32)
    output_sum = jnp.zeros(output_full.shape, jnp.float32)
    gain_one = jnp.zeros(norm_full.shape[1:], jnp.float32)
    shift_one = jnp.zeros(norm_full.shape[1:], jnp.float32)
    input_grads = []
    for cell_index in range(cell_count):
        grad_input, attend_grad, output_grad, gain_grad, shift_grad = attention_back(
            middle_grads[cell_index],
            attend_states[cell_index],
            norm_full[0],
            attend_full,
            output_full,
            valid_masks[cell_index],
        )
        attend_sum = attend_sum + attend_grad
        output_sum = output_sum + output_grad
        gain_one = gain_one + gain_grad
        shift_one = shift_one + shift_grad
        input_grads.append(grad_input)
    attend_reduced, output_reduced, expand_reduced, reduce_reduced = (
        lax.psum_scatter(attend_sum, "dp", scatter_dimension=1, tiled=True),
        lax.psum_scatter(output_sum, "dp", scatter_dimension=1, tiled=True),
        lax.psum_scatter(expand_sum, "dp", scatter_dimension=0, tiled=True),
        lax.psum_scatter(reduce_sum, "dp", scatter_dimension=1, tiled=True),
    )
    norm_grad = jnp.stack([gain_one, shift_one, gain_two, shift_two])
    norm_reduced = lax.psum_scatter(norm_grad, ("dp", "mp"), scatter_dimension=1, tiled=True)
    step_number = step_count[0].astype(jnp.float32)
    norm_new = adam_step(
        norm_params, norm_first, norm_second, norm_reduced, norm_rate, 0.0, step_number
    )
    attend_new = adam_step(
        attend_weight,
        attend_first,
        attend_second,
        attend_reduced,
        2.0 * D ** (-0.5),
        decay_rate,
        step_number,
    )
    output_new = adam_step(
        output_weight,
        output_first,
        output_second,
        output_reduced,
        2.0 * (2 * D // SEQ) ** (-0.5),
        decay_rate,
        step_number,
    )
    expand_new = adam_step(
        expand_weight,
        expand_first,
        expand_second,
        expand_reduced,
        2.0 * D ** (-0.5),
        decay_rate,
        step_number,
    )
    reduce_new = adam_step(
        reduce_weight,
        reduce_first,
        reduce_second,
        reduce_reduced,
        2.0 * FF ** (-0.5),
        decay_rate,
        step_number,
    )
    return (
        jnp.stack(results),
        jnp.stack(input_grads),
        norm_new[0],
        norm_new[1],
        norm_new[2][0:2],
        norm_new[2][2:4],
        attend_new[0],
        attend_new[1],
        attend_new[2],
        output_new[0],
        output_new[1],
        output_new[2],
        expand_new[0],
        expand_new[1],
        expand_new[2],
        reduce_new[0],
        reduce_new[1],
        reduce_new[2],
    )


def solution(mesh):
    return jax.shard_map(
        per_device,
        mesh=mesh,
        in_specs=(
            P("dp", "mp", None),
            P("dp", "mp", None),
            P("dp"),
            P(),
            P(None, ("dp", "mp")),
            P(None, ("dp", "mp")),
            P(None, ("dp", "mp")),
            P(None, "dp", "mp"),
            P(None, "dp", "mp"),
            P(None, "dp", "mp"),
            P("mp", "dp"),
            P("mp", "dp"),
            P("mp", "dp"),
            P("dp", "mp"),
            P("dp", "mp"),
            P("dp", "mp"),
            P("mp", "dp"),
            P("mp", "dp"),
            P("mp", "dp"),
        ),
        out_specs=(
            P("dp", "mp", None),
            P("dp", "mp", None),
            P(None, ("dp", "mp")),
            P(None, ("dp", "mp")),
            P(None, ("dp", "mp")),
            P(None, ("dp", "mp")),
            P(None, "dp", "mp"),
            P(None, "dp", "mp"),
            P(None, "dp", "mp"),
            P("mp", "dp"),
            P("mp", "dp"),
            P("mp", "dp"),
            P("dp", "mp"),
            P("dp", "mp"),
            P("dp", "mp"),
            P("mp", "dp"),
            P("mp", "dp"),
            P("mp", "dp"),
        ),
        check_vma=False,
    )
```

profile of v0, /device:TPU:1, one launch (start us, length us, event | category | flops | bytes accessed | tf_op | source)
XLA Modules:
  0.0 1725.8 jit_solution(1597166177206007736)
XLA Ops:
  10.7 65.2 %all-gather.2 = f32[32,40,4]{1,2,0:T(4,128)S(1)} all-gather(f32[1,40,4]{1,2,0:T(4,128)} %bitcast.322), channel_id=1, replica_groups=mesh['dp'=8,'mp'=4] {'dp','mp'}, dimensions={0}, use_global_device_ids=true | all-gather | bytes 21120 | tf_op jit(solution)/shard_map/all_gather | solution.py:238
  97.4 38.0 %all-gather.25.cloned.1.call-done = bf16[1024,1280]{1,0:T(8,128)(2,1)} async-done(((bf16[256,1280]{1,0:T(8,128)(2,1)}), bf16[1024,1280]{1,0:T(8,128)(2,1)}) %all-gather.25.cloned.1.call-update) | async-done | bytes 2621456 | tf_op jit(solution)/shard_map/all_gather | solution.py:54
  135.4 33.2 %all-gather.17.cloned.1.call-done = bf16[3,1280,320]{2,1,0:T(8,128)(2,1)} async-done(((bf16[3,160,320]{2,1,0:T(8,128)(2,1)}), bf16[3,1280,320]{2,1,0:T(8,128)(2,1)}) %all-gather.17.cloned.1.call-update) | async-done | bytes 2457616 | tf_op jit(solution)/shard_map/all_gather | solution.py:240
  196.7 28.5 %all-gather.15.cloned.1.call-done = bf16[1024,1280]{1,0:T(8,128)(2,1)} async-done(((bf16[256,1280]{1,0:T(8,128)(2,1)}), bf16[1024,1280]{1,0:T(8,128)(2,1)}) %all-gather.15.cloned.1.call-update) | async-done | bytes 2621456 | tf_op jit(solution)/shard_map/all_gather | solution.py:54
  253.6 66.4 %reduce-scatter.20.cloned.1.call-done = f32[256,1280]{1,0:T(8,128)} async-done(((f32[1024,1280]{1,0:T(8,128)}), f32[256,1280]{1,0:T(8,128)}) %reduce-scatter.20.cloned.1.call-update) | async-done | bytes 1310736 | tf_op jit(solution)/shard_map/reduce_scatter | solution.py:58
  320.0 96.4 %reduce-scatter.16.cloned.1.call-done = f32[256,1280]{1,0:T(8,128)} async-done(((f32[1024,1280]{1,0:T(8,128)}), f32[256,1280]{1,0:T(8,128)}) %reduce-scatter.16.cloned.1.call-update) | async-done | bytes 1310736 | tf_op jit(solution)/shard_map/reduce_scatter | solution.py:58
  423.8 28.8 %all-gather.21.cloned.1.call-done = bf16[1280,1280]{1,0:T(8,128)(2,1)} async-done(((bf16[160,1280]{1,0:T(8,128)(2,1)}), bf16[1280,1280]{1,0:T(8,128)(2,1)}) %all-gather.21.cloned.1.call-update) | async-done | bytes 3276816 | tf_op jit(solution)/shard_map/all_gather | solution.py:242
  452.5 56.5 %all-gather.19.cloned.1.call-done = bf16[1024,1280]{1,0:T(8,128)(2,1)} async-done(((bf16[256,1280]{1,0:T(8,128)(2,1)}), bf16[1024,1280]{1,0:T(8,128)(2,1)}) %all-gather.19.cloned.1.call-update) | async-done | bytes 2621456 | tf_op jit(solution)/shard_map/all_gather | solution.py:54
  509.1 18.3 %multiply_convert_fusion.5 = (bf16[1024,1280]{1,0:T(8,128)(2,1)}, f32[1024,1280]{1,0:T(8,128)}, f32[1024,1280]{1,0:T(8,128)}) fusion(bf16[1024,1280]{1,0:T(8,128)(2,1)} %all-gather.19.cloned.1.call-done, bf16[1280,1280]{1,0:T(8,128)(2,1)} %all-gather.21.cloned.1.call-done), kind=kOutput, calls=%fused_computation.61 | convolution fusion | flops 3440640000 | bytes 19005440 | tf_op jit(solution)/shard_map/dot_general | solution.py:187
  527.3 37.5 %all-gather.33.cloned.1.call-done = bf16[1,1024,1280]{2,1,0:T(8,128)(2,1)} async-done(((bf16[1,256,1280]{2,1,0:T(8,128)(2,1)}), bf16[1,1024,1280]{2,1,0:T(8,128)(2,1)}) %all-gather.33.cloned.1.call-update) | async-done | bytes 2621456 | tf_op jit(solution)/shard_map/all_gather | solution.py:62
  573.9 46.7 %all-gather.27.cloned.1.call-done = bf16[1024,1280]{1,0:T(8,128)(2,1)} async-done(((bf16[256,1280]{1,0:T(8,128)(2,1)}), bf16[1024,1280]{1,0:T(8,128)(2,1)}) %all-gather.27.cloned.1.call-update) | async-done | bytes 2621456 | tf_op jit(solution)/shard_map/all_gather | solution.py:54
  638.0 38.2 %all-gather.35.cloned.1.call-done = bf16[1,1024,1280]{2,1,0:T(8,128)(2,1)} async-done(((bf16[1,256,1280]{2,1,0:T(8,128)(2,1)}), bf16[1,1024,1280]{2,1,0:T(8,128)(2,1)}) %all-gather.35.cloned.1.call-update) | async-done | bytes 2621456 | tf_op jit(solution)/shard_map/all_gather | solution.py:62
  688.0 61.0 %reduce-scatter.36.cloned.1.call-done = f32[1280,160]{0,1:T(8,128)} async-done(((f32[1280,1280]{0,1:T(8,128)}), f32[1280,160]{0,1:T(8,128)}) %reduce-scatter.36.cloned.1.call-update) | async-done | bytes 819216 | tf_op jit(solution)/shard_map/reduce_scatter | solution.py:310
  752.4 33.2 %all-gather.23.cloned.1.call-done = bf16[1280,1280]{0,1:T(8,128)(2,1)} async-done(((bf16[1280,160]{0,1:T(8,128)(2,1)}), bf16[1280,1280]{0,1:T(8,128)(2,1)}) %all-gather.23.cloned.1.call-update) | async-done | bytes 3276816 | tf_op jit(solution)/shard_map/all_gather | solution.py:243
  837.9 58.5 %reduce-scatter.24.cloned.1.call-done = f32[256,1280]{1,0:T(8,128)} async-done(((f32[1024,1280]{1,0:T(8,128)}), f32[256,1280]{1,0:T(8,128)}) %reduce-scatter.24.cloned.1.call-update) | async-done | bytes 1310736 | tf_op jit(solution)/shard_map/reduce_scatter | solution.py:66
  896.4 96.6 %reduce-scatter.28.cloned.1.call-done = f32[256,1280]{1,0:T(8,128)} async-done(((f32[1024,1280]{1,0:T(8,128)}), f32[256,1280]{1,0:T(8,128)}) %reduce-scatter.28.cloned.1.call-update) | async-done | bytes 1310736 | tf_op jit(solution)/shard_map/reduce_scatter | solution.py:66
  996.5 93.1 %reduce-scatter.18.cloned.1.call-done = f32[256,1280]{1,0:T(8,128)} async-done(((f32[1024,1280]{1,0:T(8,128)}), f32[256,1280]{1,0:T(8,128)}) %reduce-scatter.18.cloned.1.call-update) | async-done | bytes 1310736 | tf_op jit(solution)/shard_map/reduce_scatter | solution.py:58
  1089.5 96.6 %reduce-scatter.22.cloned.1.call-done = f32[256,1280]{1,0:T(8,128)} async-done(((f32[1024,1280]{1,0:T(8,128)}), f32[256,1280]{1,0:T(8,128)}) %reduce-scatter.22.cloned.1.call-update) | async-done | bytes 1310736 | tf_op jit(solution)/shard_map/reduce_scatter | solution.py:58
  1204.2 42.4 %all-gather.29.cloned.1.call-done = bf16[1024,1280]{1,0:T(8,128)(2,1)} async-done(((bf16[256,1280]{1,0:T(8,128)(2,1)}), bf16[1024,1280]{1,0:T(8,128)(2,1)}) %all-gather.29.cloned.1.call-update) | async-done | bytes 2621456 | tf_op jit(solution)/shard_map/all_gather | solution.py:62
  1272.5 19.2 %multiply_convert_fusion.2 = (bf16[5,512,1024]{2,1,0:T(8,128)(2,1)}, bf16[5,512,1024]{2,1,0:T(8,128)(2,1)}) fusion(f32[5,512,1024]{2,1,0:T(8,128)} %get-tuple-element.180, f32[5,512]{1,0:T(8,128)S(1)} %get-tuple-element.98, f32[5,512]{1,0:T(8,128)S(1)} %log_add_fusion.2, f32[5,512,1024]{2,1,0:T(8,128)} %copy-done.1, pred[1024]{0:T(1024)(128)(4,1)S(1)} %copy-done.92, ...), kind=kLoop, calls=%fused_computation.6 | loop fusion | flops 31457280 | bytes 52470784 | tf_op jit(solution)/shard_map/convert_element_type | solution.py:118
  1442.6 34.7 %reduce-scatter.38.cloned.1.call-done = f32[160,960]{1,0:T(8,128)} async-done(((f32[1280,960]{1,0:T(8,128)}), f32[160,960]{1,0:T(8,128)}) %reduce-scatter.38.cloned.1.call-update) | async-done | bytes 614416
  1482.9 90.5 %reduce-scatter.26.cloned.1.call-done = f32[256,1280]{1,0:T(8,128)} async-done(((f32[1024,1280]{1,0:T(8,128)}), f32[256,1280]{1,0:T(8,128)}) %reduce-scatter.26.cloned.1.call-update) | async-done | bytes 1310736 | tf_op jit(solution)/shard_map/reduce_scatter | solution.py:66
  1573.4 96.6 %reduce-scatter.30.cloned.1.call-done = f32[256,1280]{1,0:T(8,128)} async-done(((f32[1024,1280]{1,0:T(8,128)}), f32[256,1280]{1,0:T(8,128)}) %reduce-scatter.30.cloned.1.call-update) | async-done | bytes 1310736 | tf_op jit(solution)/shard_map/reduce_scatter | solution.py:66
  1673.0 40.2 %all-reduce = f32[4,1280]{1,0:T(4,128)S(1)} all-reduce(f32[4,1280]{1,0:T(4,128)S(1)} %pad_maximum_fusion.12), channel_id=12, replica_groups=mesh['dp'=8,'mp'=4] {'dp','mp'}, use_global_device_ids=true, to_apply=%region_44.45.clone | all-reduce | flops 5120 | bytes 40960
  (444 shorter events, 391.3 us)
Async XLA Ops:
  7.2 128.2 %all-gather.25.cloned.1.call-start = ((), (), s32[]{:S(2)}) async-start(), calls=%async_computation.19 | async-start | bytes 3276800 | tf_op jit(solution)/shard_map/all_gather | solution.py:54
  76.1 343.1 %copy-start.67 = (f32[1280]{0:T(1024)}, f32[1280]{0:T(1024)S(1)}, u32[]{:S(2)}) copy-start(f32[1280]{0:T(1024)S(1)} %get-tuple-element.94) | copy-start | bytes 15364
  79.5 89.1 %all-gather.17.cloned.1.call-start = ((), (), s32[]{:S(2)}) async-start(), calls=%async_computation.13 | async-start | bytes 3317760 | tf_op jit(solution)/shard_map/all_gather | solution.py:240
  80.4 144.8 %all-gather.15.cloned.1.call-start = ((), (), s32[]{:S(2)}) async-start(), calls=%async_computation.12 | async-start | bytes 3276800 | tf_op jit(solution)/shard_map/all_gather | solution.py:54
  81.1 238.8 %reduce-scatter.20.cloned.1.call-start = ((), (), s32[]{:S(2)}) async-start(), calls=%async_computation.20 | async-start | bytes 6553600 | tf_op jit(solution)/shard_map/reduce_scatter | solution.py:58
  195.7 220.7 %reduce-scatter.16.cloned.1.call-start = ((), (), s32[]{:S(2)}) async-start(), calls=%async_computation.14 | async-start | bytes 6553600 | tf_op jit(solution)/shard_map/reduce_scatter | solution.py:58
  252.2 200.3 %all-gather.21.cloned.1.call-start = ((), (), s32[]{:S(2)}) async-start(), calls=%async_computation.16 | async-start | bytes 3686400 | tf_op jit(solution)/shard_map/all_gather | solution.py:242
  253.1 256.0 %all-gather.19.cloned.1.call-start = ((), (), s32[]{:S(2)}) async-start(), calls=%async_computation.15 | async-start | bytes 3276800 | tf_op jit(solution)/shard_map/all_gather | solution.py:54
  421.2 143.7 %all-gather.33.cloned.1.call-start = ((), (), s32[]{:S(2)}) async-start(), calls=%async_computation.32 | async-start | bytes 3276800 | tf_op jit(solution)/shard_map/all_gather | solution.py:62
  422.4 198.2 %all-gather.27.cloned.1.call-start = ((), (), s32[]{:S(2)}) async-start(), calls=%async_computation.21 | async-start | bytes 3276800 | tf_op jit(solution)/shard_map/all_gather | solution.py:54
  423.1 253.0 %all-gather.35.cloned.1.call-start = ((), (), s32[]{:S(2)}) async-start(), calls=%async_computation.33 | async-start | bytes 3276800 | tf_op jit(solution)/shard_map/all_gather | solution.py:62
  423.7 325.3 %reduce-scatter.36.cloned.1.call-start = ((), (), s32[]{:S(2)}) async-start(), calls=%async_computation.31 | async-start | bytes 7372800 | tf_op jit(solution)/shard_map/reduce_scatter | solution.py:310
  687.0 98.5 %all-gather.23.cloned.1.call-start = ((), (), s32[]{:S(2)}) async-start(), calls=%async_computation.17 | async-start | bytes 3686400 | tf_op jit(solution)/shard_map/all_gather | solution.py:243
  752.1 144.3 %reduce-scatter.24.cloned.1.call-start = ((), (), s32[]{:S(2)}) async-start(), calls=%async_computation.23 | async-start | bytes 6553600 | tf_op jit(solution)/shard_map/reduce_scatter | solution.py:66
  802.9 190.1 %reduce-scatter.28.cloned.1.call-start = ((), (), s32[]{:S(2)}) async-start(), calls=%async_computation.26 | async-start | bytes 6553600 | tf_op jit(solution)/shard_map/reduce_scatter | solution.py:66
  820.0 269.5 %reduce-scatter.18.cloned.1.call-start = ((), (), s32[]{:S(2)}) async-start(), calls=%async_computation.18 | async-start | bytes 6553600 | tf_op jit(solution)/shard_map/reduce_scatter | solution.py:58
  829.7 356.4 %reduce-scatter.22.cloned.1.call-start = ((), (), s32[]{:S(2)}) async-start(), calls=%async_computation.22 | async-start | bytes 6553600 | tf_op jit(solution)/shard_map/reduce_scatter | solution.py:58
  837.9 408.8 %all-gather.29.cloned.1.call-start = ((), (), s32[]{:S(2)}) async-start(), calls=%async_computation.24 | async-start | bytes 3276800 | tf_op jit(solution)/shard_map/all_gather | solution.py:62
  1191.2 111.1 %all-gather.31.cloned.1.call-start = ((), (), s32[]{:S(2)}) async-start(), calls=%async_computation.27 | async-start | bytes 3276800 | tf_op jit(solution)/shard_map/all_gather | solution.py:62
  1191.8 241.7 %reduce-scatter.34.cloned.1.call-start = ((), (), s32[]{:S(2)}) async-start(), calls=%async_computation.30 | async-start | bytes 7372800 | tf_op jit(solution)/shard_map/reduce_scatter | solution.py:309
  1204.2 236.1 %reduce-scatter.32.cloned.1.call-start = ((), (), s32[]{:S(2)}) async-start(), calls=%async_computation.29 | async-start | bytes 2211840 | tf_op jit(solution)/shard_map/reduce_scatter | solution.py:308
  1376.9 100.4 %reduce-scatter.38.cloned.1.call-start = ((), (), s32[]{:S(2)}) async-start(), calls=%async_computation.34 | async-start | bytes 5898240
  1416.7 156.8 %reduce-scatter.26.cloned.1.call-start = ((), (), s32[]{:S(2)}) async-start(), calls=%async_computation.25 | async-start | bytes 6553600 | tf_op jit(solution)/shard_map/reduce_scatter | solution.py:66
  1425.0 245.0 %reduce-scatter.30.cloned.1.call-start = ((), (), s32[]{:S(2)}) async-start(), calls=%async_computation.28 | async-start | bytes 6553600 | tf_op jit(solution)/shard_map/reduce_scatter | solution.py:66
  (133 other events, 7529.8 us)
Sparse Core Ops, SparseCore 0:
  79.7 55.6 all-gather.24
  137.9 30.7 all-gather.16
  170.8 54.3 all-gather.14
  227.3 92.6 reduce-scatter.19
  322.1 94.2 reduce-scatter.15
  418.7 33.7 all-gather.20
  454.7 54.3 all-gather.18
  511.2 53.5 all-gather.32
  567.0 53.5 all-gather.26
  622.6 53.5 all-gather.34
  687.2 61.7 reduce-scatter.35
  752.3 33.2 all-gather.22
  803.0 93.3 reduce-scatter.23
  898.7 94.2 reduce-scatter.27
  995.2 94.2 reduce-scatter.17
  1091.8 94.2 reduce-scatter.21
  1191.4 55.2 all-gather.28
  1248.7 53.5 all-gather.30
  1306.2 61.8 reduce-scatter.33
  1377.0 39.8 reduce-scatter.31
  1420.7 56.5 reduce-scatter.37
  1479.6 93.7 reduce-scatter.25
  1575.8 94.2 reduce-scatter.29
where the time goes:
time: 1740 us; the launch traced here: 1730 us
  waiting for transfers between devices  1190 us (68%)
  matrix products  272 us (16%)
  blocking collectives  120 us (7%)
  other arithmetic  87.6 us (5%)
  local copies, waits for them, and re-layouts  37.9 us (2%)
  between operations  18.4 us (1%)
    reduce_scatter x4, waiting for transfers between devices, reduce_rows(): return lax.psum_scatter(values, 'mp', scatter_dimension=0, tiled=True)  353 us
    reduce_scatter x4, waiting for transfers between devices, reduce_grads(): return lax.psum_scatter(values, 'mp', scatter_dimension=0, tiled=True)  342 us
    all_gather x4, waiting for transfers between devices, gather_rows(): return lax.all_gather(values, 'mp', axis=0, tiled=True)  170 us
    all_gather x4, waiting for transfers between devices, gather_grads(): return lax.all_gather(values, 'mp', axis=0, tiled=True)  129 us
    all_gather x1, blocking collectives, per_device(): norm_full = lax.all_gather(norm_params, ('dp', 'mp'), axis=1, tiled=True)  65.2 us
    reduce_scatter x1, waiting for transfers between devices, per_device(): lax.psum_scatter(reduce_sum, 'dp', scatter_dimension=1, tiled=True)  61 us
    dot_general x4, matrix products, attend_back(): jnp.einsum('qhd,khd->hqk', grad_block, value_heads, preferred_element_typ...  47.6 us
    unnamed x1, blocking collectives  40.2 us
  transfers between devices with their start and end apart: 23, of which 21 were waited for; matrix products, arithmetic and copies ran while one was open for 19% of the time, Pallas kernels for 0%

commit v1 on v0

v1 whole, which is shorter than its diff:
```python
import functools

import jax
import jax.numpy as jnp
from jax import lax
from jax.experimental import pallas as pl
from jax.experimental.pallas import tpu as pltpu
from jax.sharding import PartitionSpec as P

D = 1280
HEAD_DIM = 64
FF = 5120
SEQ = 1024

eps_norm = 1e-05
masked_score = -1e30
beta_one = 0.9
beta_two = 0.95
eps_adam = 1e-08
decay_rate = 0.1
norm_rate = 0.6

F32 = jnp.float32
BF16 = jnp.bfloat16
AXES = ("dp", "mp")


def exact_gelu(values):
    return jax.nn.gelu(values, approximate=False)


def mm(left, right, dims):
    return lax.dot_general(left, right, (dims, ((), ())), preferred_element_type=F32)


def mm_nn(left, right):
    return mm(left, right, ((1,), (0,)))


def mm_nt(left, right):
    return mm(left, right, ((1,), (1,)))


def mm_tn(left, right):
    return mm(left, right, ((0,), (0,)))


def normalize(token_rows, norm_gain, norm_shift):
    mean_row = jnp.mean(token_rows, axis=-1, keepdims=True)
    centred = token_rows - mean_row
    inv_std = lax.rsqrt(jnp.mean(centred * centred, axis=-1, keepdims=True) + eps_norm)
    scaled = centred * inv_std
    return (scaled * norm_gain + norm_shift, scaled, inv_std)


def normalize_back(grad_out, scaled, inv_std, norm_gain):
    grad_scaled = grad_out * norm_gain
    centre_part = jnp.mean(grad_scaled, axis=-1, keepdims=True)
    along_part = scaled * jnp.mean(grad_scaled * scaled, axis=-1, keepdims=True)
    grad_in = inv_std * (grad_scaled - centre_part - along_part)
    return (grad_in, jnp.sum(grad_out * scaled, axis=0), jnp.sum(grad_out, axis=0))


def adam_step(weight, first_moment, second_moment, gradient, rate, decay, step_number):
    first_new = beta_one * first_moment + (1.0 - beta_one) * gradient
    second_new = beta_two * second_moment + (1.0 - beta_two) * gradient * gradient
    corr_one = 1.0 - jnp.power(beta_one, step_number)
    corr_two = 1.0 - jnp.power(beta_two, step_number)
    update = first_new / corr_one / (jnp.sqrt(second_new / corr_two) + eps_adam)
    return (weight - rate * (update + decay * weight), first_new, second_new)


def attend_kernel(heads, block, bias_ref, q_ref, kv_ref, ctx_ref, lse_ref):
    width = heads * HEAD_DIM
    bias = bias_ref[...]
    for h in range(heads):
        lo = h * HEAD_DIM
        q = q_ref[0, :, lo : lo + HEAD_DIM] * jnp.asarray(HEAD_DIM**-0.5, BF16)
        k = kv_ref[0, :, width + lo : width + lo + HEAD_DIM]
        v = kv_ref[0, :, 2 * width + lo : 2 * width + lo + HEAD_DIM]
        s = mm_nt(q, k) + bias
        top = jnp.max(s, axis=-1, keepdims=True)
        e = jnp.exp(s - top)
        total = jnp.sum(e, axis=-1, keepdims=True)
        ctx = mm_nn(e.astype(BF16), v) / total
        ctx_ref[0, :, lo : lo + HEAD_DIM] = ctx.astype(BF16)
        lse_ref[0, :, h : h + 1] = top + jnp.log(total)


def attend(qkv, bias, heads):
    chunks, seq, _ = qkv.shape
    block = min(256, seq)
    width = heads * HEAD_DIM
    return pl.pallas_call(
        functools.partial(attend_kernel, heads, block),
        grid=(chunks, seq // block),
        in_specs=[
            pl.BlockSpec((1, seq), lambda i, j: (0, 0)),
            pl.BlockSpec((1, block, 3 * width), lambda i, j: (i, j, 0)),
            pl.BlockSpec((1, seq, 3 * width), lambda i, j: (i, 0, 0)),
        ],
        out_specs=[
            pl.BlockSpec((1, block, width), lambda i, j: (i, j, 0)),
            pl.BlockSpec((1, block, 8), lambda i, j: (i, j, 0)),
        ],
        out_shape=[
            jax.ShapeDtypeStruct((chunks, seq, width), BF16),
            jax.ShapeDtypeStruct((chunks, seq, 8), F32),
        ],
        cost_estimate=pl.CostEstimate(
            flops=16 * chunks * heads * seq * seq * HEAD_DIM,
            bytes_accessed=8 * chunks * seq * width,
            transcendentals=chunks * heads * seq * seq,
        ),
        name="attend",
    )(bias, qkv, qkv)


def attend_back_kernel(heads, bias_ref, q_ref, g_ref, o_ref, lse_ref, kv_ref, gq_ref, gkv_ref, acc_ref):
    width = heads * HEAD_DIM
    step = pl.program_id(1)
    scale = HEAD_DIM**-0.5

    @pl.when(step == 0)
    def _():
        acc_ref[...] = jnp.zeros_like(acc_ref)

    bias = bias_ref[...]
    lse_rows = lse_ref[0].T
    for h in range(heads):
        lo = h * HEAD_DIM
        q = q_ref[0, :, lo : lo + HEAD_DIM] * jnp.asarray(scale, BF16)
        g = g_ref[0, :, lo : lo + HEAD_DIM]
        o = o_ref[0, :, lo : lo + HEAD_DIM]
        k = kv_ref[0, :, width + lo : width + lo + HEAD_DIM]
        v = kv_ref[0, :, 2 * width + lo : 2 * width + lo + HEAD_DIM]
        delta = jnp.sum(g.astype(F32) * o.astype(F32), axis=-1, keepdims=True).T
        st = mm_nt(k, q) + bias
        pt = jnp.exp(st - lse_rows[h : h + 1, :])
        gpt = mm_nt(v, g)
        gst = (pt * (gpt - delta)).astype(BF16)
        acc_ref[:, width + lo : width + lo + HEAD_DIM] += mm_nn(pt.astype(BF16), g)
        acc_ref[:, lo : lo + HEAD_DIM] += mm_nn(gst, q)
        gq_ref[0, :, lo : lo + HEAD_DIM] = (mm_tn(gst, k) * scale).astype(BF16)

    @pl.when(step == pl.num_programs(1) - 1)
    def _():
        gkv_ref[0] = acc_ref[...].astype(BF16)


def attend_back(qkv, grad_ctx, ctx, lse, bias_col, heads):
    chunks, seq, _ = qkv.shape
    block = min(256, seq)
    width = heads * HEAD_DIM
    return pl.pallas_call(
        functools.partial(attend_back_kernel, heads),
        grid=(chunks, seq // block),
        in_specs=[
            pl.BlockSpec((seq, 1), lambda i, j: (0, 0)),
            pl.BlockSpec((1, block, 3 * width), lambda i, j: (i, j, 0)),
            pl.BlockSpec((1, block, width), lambda i, j: (i, j, 0)),
            pl.BlockSpec((1, block, width), lambda i, j: (i, j, 0)),
            pl.BlockSpec((1, block, 8), lambda i, j: (i, j, 0)),
            pl.BlockSpec((1, seq, 3 * width), lambda i, j: (i, 0, 0)),
        ],
        out_specs=[
            pl.BlockSpec((1, block, width), lambda i, j: (i, j, 0)),
            pl.BlockSpec((1, seq, 2 * width), lambda i, j: (i, 0, 0)),
        ],
        out_shape=[
            jax.ShapeDtypeStruct((chunks, seq, width), BF16),
            jax.ShapeDtypeStruct((chunks, seq, 2 * width), BF16),
        ],
        scratch_shapes=[pltpu.VMEM((seq, 2 * width), F32)],
        cost_estimate=pl.CostEstimate(
            flops=40 * chunks * heads * seq * seq * HEAD_DIM,
            bytes_accessed=20 * chunks * seq * width,
            transcendentals=chunks * heads * seq * seq,
        ),
        name="attend_back",
    )(bias_col, qkv, grad_ctx, ctx, lse, qkv)


class Routes:
    def __init__(self, dp_size, mp_size):
        self.dp, self.mp = dp_size, mp_size
        self.bits = (dp_size // 2).bit_length() - 1
        self.mp_bits = mp_size.bit_length() - 1

    def _pairs(self, target):
        pairs = []
        for d in range(self.dp):
            for m in range(self.mp):
                dest = target(d // 2, d % 2, m)
                pairs.append((d * self.mp + m, (dest[0] * 2 + dest[1]) * self.mp + dest[2]))
        return pairs

    def send(self, value, target, back=False):
        pairs = self._pairs(target)
        if back:
            pairs = [(b, a) for a, b in pairs]
        return lax.ppermute(value, AXES, pairs)

    def partner(self, value):
        return self.send(value, lambda p, c, m: (p, 1 - c, m))

    def pair_bit(self, value, bit):
        return self.send(value, lambda p, c, m: (p ^ (1 << bit), c, m))

    def mp_bit(self, value, bit):
        return self.send(value, lambda p, c, m: (p, c, m ^ (1 << bit)))

    def cell(self, value, k, back=False):
        return self.send(value, lambda p, c, m: (p, m // 2, 2 * c + ((m % 2) ^ k)), back)

    def shard(self, value, k, back=False):
        return self.send(value, lambda p, c, m: (p, m // 2, m ^ k ^ (2 * c)), back)


def gather_shards(routes, shard):
    got = [routes.shard(shard, k) for k in range(4)]
    chunks = []
    for half in range(2):
        own = jnp.stack([got[half], got[half + 2]])
        order = range(routes.bits) if half else reversed(range(routes.bits))
        pieces = {0: own}
        for bit in order:
            if routes.bits <= 2:
                pieces.update({r | (1 << bit): routes.pair_bit(v, bit) for r, v in list(pieces.items())})
            else:
                keys = sorted(pieces)
                cat = routes.pair_bit(jnp.stack([pieces[r] for r in keys]), bit)
                pieces.update({r | (1 << bit): cat[i] for i, r in enumerate(keys)})
        chunks.append(pieces)
    return chunks


def assemble(pieces, mask):
    count = len(pieces)
    _, rows, width = pieces[0].shape
    full = jnp.zeros((count * 2 * rows, width), pieces[0].dtype)
    for r in range(count):
        for e in range(2):
            full = lax.dynamic_update_slice(full, pieces[r][e], ((((2 * r + e) ^ mask)) * rows, 0))
    return full


def scatter_grads(routes, chunks, mask):
    partial = []
    for half in range(2):
        full = chunks[half]
        count = 1 << routes.bits
        rows = full.shape[0] // (2 * count)
        blocks = full.reshape(2 * count, rows, full.shape[1])
        pieces = {
            r: jnp.stack([lax.dynamic_index_in_dim(blocks, (2 * r + e) ^ mask, 0, keepdims=False) for e in range(2)])
            for r in range(count)
        }
        order = range(routes.bits) if not half else reversed(range(routes.bits))
        for bit in order:
            keys = sorted(r for r in pieces if not r & (1 << bit))
            sent = routes.pair_bit(jnp.stack([pieces[r | (1 << bit)] for r in keys]), bit)
            pieces = {
                r: (pieces[r].astype(F32) + sent[i].astype(F32)).astype(BF16) for i, r in enumerate(keys)
            }
        partial.append(pieces[0])
    total = None
    for k in range(4):
        got = routes.shard(partial[k % 2][k // 2], k, back=True).astype(F32)
        total = got if total is None else total + got
    return total


def gather_norms(routes, norm_params, d, m):
    cur = norm_params
    for bit in range(routes.mp_bits):
        got = routes.mp_bit(cur, bit)
        high = ((m >> bit) & 1) == 1
        cur = jnp.where(high, jnp.concatenate([got, cur], 1), jnp.concatenate([cur, got], 1))
    for bit in range(routes.bits + 1):
        got = routes.partner(cur) if bit == 0 else routes.pair_bit(cur, bit - 1)
        high = ((d >> bit) & 1) == 1
        cur = jnp.where(high, jnp.concatenate([got, cur], 1), jnp.concatenate([cur, got], 1))
    return cur


def scatter_norms(routes, grads, d, m):
    cur = grads
    for bit in reversed(range(routes.bits + 1)):
        low, up = jnp.split(cur, 2, axis=1)
        high = ((d >> bit) & 1) == 1
        give = jnp.where(high, low, up)
        got = routes.partner(give) if bit == 0 else routes.pair_bit(give, bit - 1)
        cur = jnp.where(high, up, low) + got
    for bit in reversed(range(routes.mp_bits)):
        low, up = jnp.split(cur, 2, axis=1)
        high = ((m >> bit) & 1) == 1
        cur = jnp.where(high, up, low) + routes.mp_bit(jnp.where(high, low, up), bit)
    return cur


def per_device(
    inputs, cotangent, gene_counts, step_count, norm_params, norm_first, norm_second,
    attend_weight, attend_first, attend_second, output_weight, output_first, output_second,
    expand_weight, expand_first, expand_second, reduce_weight, reduce_first, reduce_second,
):
    routes = Routes(lax.axis_size("dp"), lax.axis_size("mp"))
    d, m = lax.axis_index("dp"), lax.axis_index("mp")
    c = d % 2
    cells, quarter, _ = inputs.shape
    assert routes.mp == 4 and 2 * cells == routes.mp and routes.dp % 2 == 0
    half = 2 * quarter
    seq = 2 * half
    heads = attend_weight.shape[2] // HEAD_DIM
    width = heads * HEAD_DIM
    m_low, m_high = m % 2, m // 2
    mask = 2 * (d // 2) + ((c + m_high) % 2)

    norm_full = gather_norms(routes, norm_params, d, m)

    def to_cell(values):
        got = [
            routes.cell(lax.dynamic_index_in_dim(values, (m_low + k) % 2, 0, keepdims=False), k) for k in range(2)
        ]
        return jnp.concatenate(got, 0)

    def from_cell(rows):
        rows = rows.astype(BF16)
        got = [routes.cell(rows[k * quarter : (k + 1) * quarter], k, back=True) for k in range(2)]
        flip = m_low == 1
        return jnp.stack([jnp.where(flip, got[1], got[0]), jnp.where(flip, got[0], got[1])]).astype(F32)

    attend_shard = jnp.concatenate(
        [attend_weight[0], attend_weight[1], attend_weight[2], output_weight.T], axis=1
    ).astype(BF16)
    expand_shard = expand_weight.astype(BF16)
    reduce_shard = reduce_weight.T.astype(BF16)

    x_mine = to_cell(inputs).astype(F32)
    attend_w = [assemble(pieces, mask) for pieces in gather_shards(routes, attend_shard)]
    expand_w = [assemble(pieces, mask) for pieces in gather_shards(routes, expand_shard)]
    reduce_w = [assemble(pieces, mask) for pieces in gather_shards(routes, reduce_shard)]
    gy_mine = to_cell(cotangent)

    other_counts = routes.partner(gene_counts)
    mine = jnp.where(m_high == c, gene_counts, other_counts)
    count = jnp.where(m_low == 1, mine[1], mine[0])
    inside = jnp.arange(quarter)
    positions = jnp.concatenate(
        [
            h * half + b * quarter + inside
            for h, b in ((c, m_low), (c, 1 - m_low), (1 - c, m_low), (1 - c, 1 - m_low))
        ]
    )
    bias = jnp.where(positions < 1 + count, 0.0, masked_score).astype(F32)

    def both(rows):
        return jnp.concatenate([rows, routes.partner(rows)], 0)

    def fold(partial):
        return partial[:half] + routes.partner(partial[half:].astype(BF16)).astype(F32)

    normed, scaled_one, inv_one = normalize(x_mine, norm_full[0], norm_full[1])
    h1 = both(normed.astype(BF16))
    qkv = jnp.stack([mm_nn(h1, w[:, : 3 * width]).astype(BF16) for w in attend_w])
    ctx, lse = attend(qkv, bias[None, :], heads)
    branch = mm_nt(ctx[0], attend_w[0][:, 3 * width :]) + mm_nt(ctx[1], attend_w[1][:, 3 * width :])
    x2 = x_mine + fold(branch)
    normed, scaled_two, inv_two = normalize(x2, norm_full[2], norm_full[3])
    h2 = both(normed.astype(BF16))
    hidden = [mm_nn(h2, w) for w in expand_w]
    active = [exact_gelu(u).astype(BF16) for u in hidden]
    branch = mm_nt(active[0], reduce_w[0]) + mm_nt(active[1], reduce_w[1])
    outputs = from_cell(x2 + fold(branch))

    gy = both(gy_mine)
    reduce_grad = [mm_tn(gy, a).astype(BF16) for a in active]
    grad_hidden = [
        jax.vjp(exact_gelu, u)[1](mm_nn(gy, w))[0].astype(BF16) for u, w in zip(hidden, reduce_w)
    ]
    expand_grad = [mm_tn(h2, g).astype(BF16) for g in grad_hidden]
    gh2 = fold(mm_nt(grad_hidden[0], expand_w[0]) + mm_nt(grad_hidden[1], expand_w[1]))
    grad_in, gain_two, shift_two = normalize_back(gh2, scaled_two, inv_two, norm_full[2])
    gx2 = gy_mine.astype(F32) + grad_in
    gb = both(gx2.astype(BF16))
    grad_ctx = jnp.stack([mm_nn(gb, w[:, 3 * width :]).astype(BF16) for w in attend_w])
    gq, gkv = attend_back(qkv, grad_ctx, ctx, lse, bias[:, None], heads)
    attend_grad = [
        jnp.concatenate(
            [mm_tn(h1, gq[i]), mm_tn(h1, gkv[i]), mm_tn(gb, ctx[i])], axis=1
        ).astype(BF16)
        for i in range(2)
    ]
    gh1 = fold(
        sum(
            mm_nt(gq[i], attend_w[i][:, :width]) + mm_nt(gkv[i], attend_w[i][:, width : 3 * width])
            for i in range(2)
        )
    )
    grad_in, gain_one, shift_one = normalize_back(gh1, scaled_one, inv_one, norm_full[0])
    input_grad = from_cell(gx2 + grad_in)

    reduce_sum = scatter_grads(routes, reduce_grad, mask)
    expand_sum = scatter_grads(routes, expand_grad, mask)
    attend_sum = scatter_grads(routes, attend_grad, mask)
    norm_sum = scatter_norms(routes, jnp.stack([gain_one, shift_one, gain_two, shift_two]), d, m)

    step_number = step_count[0].astype(F32)
    norm_new = adam_step(norm_params, norm_first, norm_second, norm_sum, norm_rate, 0.0, step_number)
    attend_reduced = jnp.stack([attend_sum[:, i * width : (i + 1) * width] for i in range(3)])
    attend_new = adam_step(
        attend_weight, attend_first, attend_second, attend_reduced, 2.0 * D ** (-0.5), decay_rate, step_number
    )
    output_new = adam_step(
        output_weight, output_first, output_second, attend_sum[:, 3 * width :].T,
        2.0 * (2 * D // SEQ) ** (-0.5), decay_rate, step_number,
    )
    expand_new = adam_step(
        expand_weight, expand_first, expand_second, expand_sum, 2.0 * D ** (-0.5), decay_rate, step_number
    )
    reduce_new = adam_step(
        reduce_weight, reduce_first, reduce_second, reduce_sum.T, 2.0 * FF ** (-0.5), decay_rate, step_number
    )
    return (
        outputs, input_grad,
        norm_new[0], norm_new[1], norm_new[2][0:2], norm_new[2][2:4],
        *attend_new, *output_new, *expand_new, *reduce_new,
    )


def solution(mesh):
    norms = P(None, ("dp", "mp"))
    attend_spec, col, row = P(None, "dp", "mp"), P("mp", "dp"), P("dp", "mp")
    tokens = P("dp", "mp", None)
    return jax.shard_map(
        per_device,
        mesh=mesh,
        in_specs=(tokens, tokens, P("dp"), P(), norms, norms, norms)
        + (attend_spec,) * 3 + (col,) * 3 + (row,) * 3 + (col,) * 3,
        out_specs=(tokens, tokens, norms, norms, norms, norms)
        + (attend_spec,) * 3 + (col,) * 3 + (row,) * 3 + (col,) * 3,
        check_vma=False,
    )
```

time: 1740 us -> 799 us (0.46)
  waiting for transfers between devices: 1190 us -> 287 us
  starting transfers between devices: 2.75 us -> 173 us
  matrix products: 272 us -> 127 us
  blocking collectives: 120 us -> 0 us
  Pallas kernels: 0 us -> 60.6 us
  local copies, waits for them, and re-layouts: 37.9 us -> 85.4 us
  other arithmetic: 87.6 us -> 46.3 us
    reduce_scatter x11 -> x0, waiting for transfers between devices: 756 us -> none  [the longest x4 353 us: reduce_rows(): return lax.psum_scatter(values, 'mp', scatter_dimension=0, tiled=True)]
    all_gather x11 -> x0, waiting for transfers between devices: 394 us -> none  [the longest x4 170 us: gather_rows(): return lax.all_gather(values, 'mp', axis=0, tiled=True)]
    ppermute x0 -> x81, waiting for transfers between devices: none -> 287 us  [send(): return lax.ppermute(value, AXES, pairs)]
    ppermute x0 -> x81, starting transfers between devices: none -> 173 us  [send(): return lax.ppermute(value, AXES, pairs)]
    dot_general x48 -> x28, matrix products: 272 us -> 127 us  [mm(): lax.dot_general(left, right, (dims, ((), ())), preferred_element_type=F32)]
    all_gather x2 -> x0, blocking collectives: 80.1 us -> none  [the longest x1 65.2 us: per_device(): norm_full = lax.all_gather(norm_params, ('dp', 'mp'), axis=1, tiled=True)]
    pallas_call x0 -> x2, Pallas kernels: none -> 60.6 us  [the longest x1 35.1 us: attend_back(): pl.pallas_call(functools.partial(attend_back_kernel, heads), grid=(chunks...]
    unnamed x1 -> x0, blocking collectives: 40.2 us -> none
  transfers between devices with their start and end apart: 23 -> 81, of which waited for: 21 -> 39; matrix products, arithmetic and copies ran while one was open for 19% -> 23% of each run, Pallas kernels for 0% -> 8%
where the time goes in v1:
time: 799 us; the launch traced here: 784 us
  waiting for transfers between devices  287 us (36%)
  starting transfers between devices  173 us (22%)
  matrix products  127 us (16%)
  local copies, waits for them, and re-layouts  85.4 us (11%)
  Pallas kernels  60.6 us (8%)
  other arithmetic  46.3 us (6%)
    ppermute x81, waiting for transfers between devices, send(): return lax.ppermute(value, AXES, pairs)  287 us
    ppermute x81, starting transfers between devices, send(): return lax.ppermute(value, AXES, pairs)  173 us
    dot_general x28, matrix products, mm(): lax.dot_general(left, right, (dims, ((), ())), preferred_element_type=F32)  127 us
    pallas_call x1, Pallas kernels, attend_back(): pl.pallas_call(functools.partial(attend_back_kernel, heads), grid=(chunks...  35.1 us
    pallas_call x1, Pallas kernels, attend(): pl.pallas_call(functools.partial(attend_kernel, heads, block), grid=(chun...  25.5 us
    dynamic_update_slice x48, local copies, waits for them, and re-layouts, assemble(): lax.dynamic_update_slice(full, pieces[r][e], ((2 * r + e ^ mask) * rows, 0))  23.7 us
    unnamed x213, local copies, waits for them, and re-layouts  17.5 us
  transfers between devices with their start and end apart: 81, of which 39 were waited for; matrix products, arithmetic and copies ran while one was open for 23% of the time, Pallas kernels for 8%

profile of v1, /device:TPU:1, one launch (start us, length us, event | category | flops | bytes accessed | tf_op | source)
XLA Modules:
  0.0 784.3 jit_solution(11473969344909974336)
XLA Ops:
  21.9 18.6 %collective-permute-done.3 = f32[4,40]{1,0:T(4,128)S(1)} collective-permute-done((f32[4,40]{1,0:T(4,128)S(1)}, f32[4,40]{1,0:T(4,128)S(1)}, u32[]{:S(2)}, u32[]{:S(2)}) %collective-permute-start.3) | collective-permute-done | bytes 672 | tf_op jit(solution)/shard_map/ppermute | solution.py:202
  71.9 14.6 %collective-permute-done.21 = bf16[160,1280]{1,0:T(8,128)(2,1)S(1)} collective-permute-done((bf16[160,1280]{1,0:T(8,128)(2,1)}, bf16[160,1280]{1,0:T(8,128)(2,1)S(1)}, u32[]{:S(2)}, u32[]{:S(2)}) %collective-permute-start.21) | collective-permute-done | bytes 409632 | tf_op jit(solution)/shard_map/ppermute | solution.py:202
  92.4 11.8 %collective-permute-done.26 = bf16[160,1280]{1,0:T(8,128)(2,1)S(1)} collective-permute-done((bf16[160,1280]{1,0:T(8,128)(2,1)}, bf16[160,1280]{1,0:T(8,128)(2,1)S(1)}, u32[]{:S(2)}, u32[]{:S(2)}) %collective-permute-start.26) | collective-permute-done | bytes 409632 | tf_op jit(solution)/shard_map/ppermute | solution.py:202
  111.9 24.6 %collective-permute-start.44 = (bf16[256,1280]{1,0:T(8,128)(2,1)S(1)}, bf16[256,1280]{1,0:T(8,128)(2,1)S(1)}, u32[]{:S(2)}, u32[]{:S(2)}) collective-permute-start(bf16[256,1280]{1,0:T(8,128)(2,1)S(1)} %copy-done.69), channel_id=1, source_target_pairs={{0,0},{1,1},{2,4},{3,5},{4,2},{5,3},{6,6},{7,7},{8,8},{9,9},{10,12... | collective-permute-start | bytes 1966088 | tf_op jit(solution)/shard_map/ppermute | solution.py:202
  143.5 19.3 %collective-permute-done = bf16[256,1280]{1,0:T(8,128)(2,1)S(1)} collective-permute-done((bf16[256,1280]{1,0:T(8,128)(2,1)}, bf16[256,1280]{1,0:T(8,128)(2,1)S(1)}, u32[]{:S(2)}, u32[]{:S(2)}) %collective-permute-start) | collective-permute-done | bytes 655392 | tf_op jit(solution)/shard_map/ppermute | solution.py:202
  166.1 10.8 %collective-permute-done.44 = bf16[256,1280]{1,0:T(8,128)(2,1)S(1)} collective-permute-done((bf16[256,1280]{1,0:T(8,128)(2,1)S(1)}, bf16[256,1280]{1,0:T(8,128)(2,1)S(1)}, u32[]{:S(2)}, u32[]{:S(2)}) %collective-permute-start.44) | collective-permute-done | bytes 655392 | tf_op jit(solution)/shard_map/ppermute | solution.py:202
  188.3 9.8 %collective-permute-done.17 = bf16[2,160,1280]{2,1,0:T(8,128)(2,1)S(1)} collective-permute-done((bf16[2,160,1280]{2,1,0:T(8,128)(2,1)S(1)}, bf16[2,160,1280]{2,1,0:T(8,128)(2,1)S(1)}, u32[]{:S(2)}, u32[]{:S(2)}) %collective-permute-start.17) | collective-permute-done | bytes 819232 | tf_op jit(solution)/shard_map/ppermute | solution.py:202
  202.3 13.4 %collective-permute-done.24 = bf16[2,160,1280]{2,1,0:T(8,128)(2,1)} collective-permute-done((bf16[2,160,1280]{2,1,0:T(8,128)(2,1)S(1)}, bf16[2,160,1280]{2,1,0:T(8,128)(2,1)}, u32[]{:S(2)}, u32[]{:S(2)}) %collective-permute-start.24) | collective-permute-done | bytes 819232 | tf_op jit(solution)/shard_map/ppermute | solution.py:202
  219.9 8.1 %collective-permute-done.29 = bf16[2,160,1280]{2,1,0:T(8,128)(2,1)} collective-permute-done((bf16[2,160,1280]{2,1,0:T(8,128)(2,1)S(1)}, bf16[2,160,1280]{2,1,0:T(8,128)(2,1)}, u32[]{:S(2)}, u32[]{:S(2)}) %collective-permute-start.29) | collective-permute-done | bytes 819232 | tf_op jit(solution)/shard_map/ppermute | solution.py:202
  236.9 12.0 %collective-permute-done.38 = bf16[2,160,1280]{2,1,0:T(8,128)(2,1)S(1)} collective-permute-done((bf16[2,160,1280]{2,1,0:T(8,128)(2,1)S(1)}, bf16[2,160,1280]{2,1,0:T(8,128)(2,1)S(1)}, u32[]{:S(2)}, u32[]{:S(2)}) %collective-permute-start.38) | collective-permute-done | bytes 819232 | tf_op jit(solution)/shard_map/ppermute | solution.py:202
  286.3 25.5 %attend.1 = (bf16[2,1024,320]{2,1,0:T(8,128)(2,1)}, f32[2,1024,8]{2,1,0:T(8,128)}) custom-call(f32[1,1024]{1,0:T(1,128)} %compare_select_fusion.bias_ref, bf16[2,1024,960]{2,1,0:T(8,128)(2,1)} %pad_maximum_fusion.q_ref.kv_ref, bf16[2,1024,960]{2,1,0:T(8,128)(2,1)} %pad_maximum_fusion.q_ref.kv_ref), custom_call_target="tpu_custom_call" | custom-call | flops 10737418240 | bytes 5242880 | tf_op jit(solution)/shard_map/attend/pallas_call | solution.py:94
  335.1 16.3 %add_convert_fusion = (bf16[1024,1280]{1,0:T(8,128)(2,1)}, f32[1024,1280]{1,0:T(8,128)S(1)}) fusion(f32[1024,1280]{1,0:T(8,128)S(1)} %fusion.135, bf16[1024,1280]{1,0:T(8,128)(2,1)S(1)} %copy-done.78, bf16[1280,1280]{1,0:T(8,128)(2,1)S(1)} %fusion.93), kind=kOutput, calls=%fused_computation.9 | convolution fusion | flops 3449815040 | bytes 19005440 | tf_op jit(solution)/shard_map/dot_general | solution.py:33
  366.3 16.1 %add_convert_fusion.1 = (bf16[1024,1280]{1,0:T(8,128)(2,1)}, f32[1024,1280]{1,0:T(8,128)S(1)}) fusion(f32[1024,1280]{1,0:T(8,128)S(1)} %fusion.136, bf16[1024,1280]{1,0:T(8,128)(2,1)S(1)} %copy-done.79, bf16[1280,1280]{1,0:T(8,128)(2,1)S(1)} %copy-done.21), kind=kOutput, calls=%fused_computation.10 | convolution fusion | flops 3449815040 | bytes 19005440 | tf_op jit(solution)/shard_map/dot_general | solution.py:33
  434.9 27.8 %collective-permute-done.65 = bf16[2,2,160,1280]{3,2,1,0:T(8,128)(2,1)S(1)} collective-permute-done((bf16[2,2,160,1280]{3,2,1,0:T(8,128)(2,1)}, bf16[2,2,160,1280]{3,2,1,0:T(8,128)(2,1)S(1)}, u32[]{:S(2)}, u32[]{:S(2)}) %collective-permute-start.65) | collective-permute-done | bytes 1638432 | tf_op jit(solution)/shard_map/ppermute | solution.py:202
  464.8 16.8 %collective-permute-done.74 = bf16[1,2,160,1280]{3,2,1,0:T(8,128)(2,1)S(1)} collective-permute-done((bf16[1,2,160,1280]{3,2,1,0:T(8,128)(2,1)S(1)}, bf16[1,2,160,1280]{3,2,1,0:T(8,128)(2,1)S(1)}, u32[]{:S(2)}, u32[]{:S(2)}) %collective-permute-start.74) | collective-permute-done | bytes 819232 | tf_op jit(solution)/shard_map/ppermute | solution.py:202
  482.9 7.9 %collective-permute-start.75 = (bf16[160,1280]{1,0:T(8,128)(2,1)}, bf16[160,1280]{1,0:T(8,128)(2,1)}, u32[]{:S(2)}, u32[]{:S(2)}) collective-permute-start(bf16[160,1280]{1,0:T(8,128)(2,1)} %get-tuple-element.122), channel_id=1, source_target_pairs={{0,0},{1,1},{6,2},{7,3},{2,4},{3,5},{4,6},{5,7},{8,8},{9,9},{14,10... | collective-permute-start | bytes 1228808 | tf_op jit(solution)/shard_map/ppermute | solution.py:202
  527.9 35.1 %attend_back.1 = (bf16[2,1024,320]{2,1,0:T(8,128)(2,1)}, bf16[2,1024,640]{2,1,0:T(8,128)(2,1)}) custom-call(f32[1024,1]{1,0:T(8,128)} %broadcast_select_fusion.bias_ref, bf16[2,1024,960]{2,1,0:T(8,128)(2,1)} %pad_maximum_fusion.q_ref.kv_ref, bf16[2,1024,320]{2,1,0:T(8,128)(2,1)} %pad_maximum_fusion.10.g_ref, bf16[2,1024,320]{2,1,0:T(8,128)(2,1)} %get-tuple-element.22.o_ref, ...), custom_call_target="tpu_custom_call" | custom-call | flops 26843545600 | bytes 13107200 | tf_op jit(solution)/shard_map/attend_back/pallas_call | solution.py:155
  599.9 7.1 concatenate.168
  644.3 7.1 collective-permute-done.70
  655.1 27.6 %collective-permute-done.52 = f32[4,640]{1,0:T(4,128)S(1)} collective-permute-done((f32[4,640]{1,0:T(4,128)S(1)}, f32[4,640]{1,0:T(4,128)S(1)}, u32[]{:S(2)}, u32[]{:S(2)}) %collective-permute-start.52) | collective-permute-done | bytes 10272 | tf_op jit(solution)/shard_map/ppermute | solution.py:202
  686.8 21.9 %collective-permute-start.55 = (f32[4,80]{1,0:T(4,128)S(1)}, f32[4,80]{1,0:T(4,128)S(1)}, u32[]{:S(2)}, u32[]{:S(2)}) collective-permute-start(f32[4,80]{1,0:T(4,128)S(1)} %slice_select_fusion.3), channel_id=1, source_target_pairs={{0,2},{1,3},{2,0},{3,1},{4,6},{5,7},{6,4},{7,5},{8,10},{9,11},{10,... | collective-permute-start | bytes 3848 | tf_op jit(solution)/shard_map/ppermute | solution.py:202
  721.3 9.6 %collective-permute-done.50 = bf16[256,1280]{1,0:T(8,128)(2,1)S(1)} collective-permute-done((bf16[256,1280]{1,0:T(8,128)(2,1)S(1)}, bf16[256,1280]{1,0:T(8,128)(2,1)S(1)}, u32[]{:S(2)}, u32[]{:S(2)}) %collective-permute-start.50) | collective-permute-done | bytes 655392 | tf_op jit(solution)/shard_map/ppermute | solution.py:202
  730.9 15.5 %collective-permute-done.51 = bf16[256,1280]{1,0:T(8,128)(2,1)S(1)} collective-permute-done((bf16[256,1280]{1,0:T(8,128)(2,1)S(1)}, bf16[256,1280]{1,0:T(8,128)(2,1)S(1)}, u32[]{:S(2)}, u32[]{:S(2)}) %collective-permute-start.51) | collective-permute-done | bytes 655392 | tf_op jit(solution)/shard_map/ppermute | solution.py:202
  764.8 10.1 %collective-permute-done.62 = bf16[160,1280]{1,0:T(8,128)(2,1)S(1)} collective-permute-done((bf16[160,1280]{1,0:T(8,128)(2,1)S(1)}, bf16[160,1280]{1,0:T(8,128)(2,1)S(1)}, u32[]{:S(2)}, u32[]{:S(2)}) %collective-permute-start.62) | collective-permute-done | bytes 409632 | tf_op jit(solution)/shard_map/ppermute | solution.py:202
  (566 shorter events, 391.4 us)
Async XLA Ops:
  3.9 52.6 %collective-permute-start.9 = (bf16[160,1280]{1,0:T(8,128)(2,1)}, bf16[160,1280]{1,0:T(8,128)(2,1)S(1)}, u32[]{:S(2)}, u32[]{:S(2)}) collective-permute-start(bf16[160,1280]{1,0:T(8,128)(2,1)} %concatenate.157), channel_id=1, source_target_pairs={{0,0},{1,1},{2,6},{3,7},{4,2},{5,3},{6,4},{7,5},{8,8},{9,9},{10,14... | collective-permute-start | bytes 1228808 | tf_op jit(solution)/shard_map/ppermute | solution.py:202
  9.5 48.9 %collective-permute-start.10 = (bf16[160,1280]{1,0:T(8,128)(2,1)}, bf16[160,1280]{1,0:T(8,128)(2,1)S(1)}, u32[]{:S(2)}, u32[]{:S(2)}) collective-permute-start(bf16[160,1280]{1,0:T(8,128)(2,1)} %concatenate.157), channel_id=1, source_target_pairs={{0,2},{1,3},{2,4},{3,5},{4,0},{5,1},{6,6},{7,7},{8,10},{9,11},{10,... | collective-permute-start | bytes 1228808 | tf_op jit(solution)/shard_map/ppermute | solution.py:202
  11.5 51.7 %collective-permute-start.14 = (bf16[160,1280]{1,0:T(8,128)(2,1)}, bf16[160,1280]{1,0:T(8,128)(2,1)S(1)}, u32[]{:S(2)}, u32[]{:S(2)}) collective-permute-start(bf16[160,1280]{1,0:T(8,128)(2,1)} %concatenate.157), channel_id=1, source_target_pairs={{0,1},{1,0},{2,7},{3,6},{4,3},{5,2},{6,5},{7,4},{8,9},{9,8},{10,15... | collective-permute-start | bytes 1228808 | tf_op jit(solution)/shard_map/ppermute | solution.py:202
  15.2 50.0 %collective-permute-start.15 = (bf16[160,1280]{1,0:T(8,128)(2,1)}, bf16[160,1280]{1,0:T(8,128)(2,1)S(1)}, u32[]{:S(2)}, u32[]{:S(2)}) collective-permute-start(bf16[160,1280]{1,0:T(8,128)(2,1)} %concatenate.157), channel_id=1, source_target_pairs={{0,3},{1,2},{2,5},{3,4},{4,1},{5,0},{6,7},{7,6},{8,11},{9,10},{10,... | collective-permute-start | bytes 1228808 | tf_op jit(solution)/shard_map/ppermute | solution.py:202
  89.9 48.3 %collective-permute-start.36 = (bf16[160,1280]{1,0:T(8,128)(2,1)}, bf16[160,1280]{1,0:T(8,128)(2,1)S(1)}, u32[]{:S(2)}, u32[]{:S(2)}) collective-permute-start(bf16[160,1280]{1,0:T(8,128)(2,1)} %convert_bitcast_fusion.2), channel_id=1, source_target_pairs={{0,1},{1,0},{2,7},{3,6},{4,3},{5,2},{6,5},{7,4},{8,9},{9,8},{10,15... | collective-permute-start | bytes 1228808 | tf_op jit(solution)/shard_map/ppermute | solution.py:202
  107.5 55.4 %collective-permute-start = (bf16[256,1280]{1,0:T(8,128)(2,1)}, bf16[256,1280]{1,0:T(8,128)(2,1)S(1)}, u32[]{:S(2)}, u32[]{:S(2)}) collective-permute-start(bf16[256,1280]{1,0:T(8,128)(2,1)} %get-tuple-element.120), channel_id=1, source_target_pairs={{0,0},{1,1},{2,4},{3,5},{4,2},{5,3},{6,6},{7,7},{8,8},{9,9},{10,12... | collective-permute-start | bytes 1966088 | tf_op jit(solution)/shard_map/ppermute | solution.py:202
  110.1 54.0 %collective-permute-start.1 = (bf16[256,1280]{1,0:T(8,128)(2,1)S(1)}, bf16[256,1280]{1,0:T(8,128)(2,1)S(1)}, u32[]{:S(2)}, u32[]{:S(2)}) collective-permute-start(bf16[256,1280]{1,0:T(8,128)(2,1)S(1)} %copy-done.70), channel_id=1, source_target_pairs={{0,1},{1,0},{2,5},{3,4},{4,3},{5,2},{6,7},{7,6},{8,9},{9,8},{10,13... | collective-permute-start | bytes 1966088 | tf_op jit(solution)/shard_map/ppermute | solution.py:202
  111.9 65.0 %collective-permute-start.44 = (bf16[256,1280]{1,0:T(8,128)(2,1)S(1)}, bf16[256,1280]{1,0:T(8,128)(2,1)S(1)}, u32[]{:S(2)}, u32[]{:S(2)}) collective-permute-start(bf16[256,1280]{1,0:T(8,128)(2,1)S(1)} %copy-done.69), channel_id=1, source_target_pairs={{0,0},{1,1},{2,4},{3,5},{4,2},{5,3},{6,6},{7,7},{8,8},{9,9},{10,12... | collective-permute-start | bytes 1966088 | tf_op jit(solution)/shard_map/ppermute | solution.py:202
  250.9 67.3 %collective-permute-start.25 = (bf16[2,160,1280]{2,1,0:T(8,128)(2,1)}, bf16[2,160,1280]{2,1,0:T(8,128)(2,1)}, u32[]{:S(2)}, u32[]{:S(2)}) collective-permute-start(bf16[2,160,1280]{2,1,0:T(8,128)(2,1)} %collective-permute-done.24), channel_id=1, source_target_pairs={{0,8},{1,9},{2,10},{3,11},{4,12},{5,13},{6,14},{7,15},{8,0},{9,1},... | collective-permute-start | bytes 2457608 | tf_op jit(solution)/shard_map/ppermute | solution.py:202
  253.4 67.0 %collective-permute-start.30 = (bf16[2,160,1280]{2,1,0:T(8,128)(2,1)}, bf16[2,160,1280]{2,1,0:T(8,128)(2,1)}, u32[]{:S(2)}, u32[]{:S(2)}) collective-permute-start(bf16[2,160,1280]{2,1,0:T(8,128)(2,1)} %collective-permute-done.29), channel_id=1, source_target_pairs={{0,8},{1,9},{2,10},{3,11},{4,12},{5,13},{6,14},{7,15},{8,0},{9,1},... | collective-permute-start | bytes 2457608 | tf_op jit(solution)/shard_map/ppermute | solution.py:202
  261.1 62.9 %collective-permute-start.35 = (bf16[2,160,1280]{2,1,0:T(8,128)(2,1)}, bf16[2,160,1280]{2,1,0:T(8,128)(2,1)}, u32[]{:S(2)}, u32[]{:S(2)}) collective-permute-start(bf16[2,160,1280]{2,1,0:T(8,128)(2,1)} %copy-done.59), channel_id=1, source_target_pairs={{0,16},{1,17},{2,18},{3,19},{4,20},{5,21},{6,22},{7,23},{8,24},{9,... | collective-permute-start | bytes 2457608 | tf_op jit(solution)/shard_map/ppermute | solution.py:202
  266.4 62.6 %collective-permute-start.40 = (bf16[2,160,1280]{2,1,0:T(8,128)(2,1)}, bf16[2,160,1280]{2,1,0:T(8,128)(2,1)}, u32[]{:S(2)}, u32[]{:S(2)}) collective-permute-start(bf16[2,160,1280]{2,1,0:T(8,128)(2,1)} %copy-done.58), channel_id=1, source_target_pairs={{0,16},{1,17},{2,18},{3,19},{4,20},{5,21},{6,22},{7,23},{8,24},{9,... | collective-permute-start | bytes 2457608 | tf_op jit(solution)/shard_map/ppermute | solution.py:202
  410.9 51.8 %collective-permute-start.65 = (bf16[2,2,160,1280]{3,2,1,0:T(8,128)(2,1)}, bf16[2,2,160,1280]{3,2,1,0:T(8,128)(2,1)S(1)}, u32[]{:S(2)}, u32[]{:S(2)}) collective-permute-start(bf16[2,2,160,1280]{3,2,1,0:T(8,128)(2,1)} %pad_maximum_fusion.6), channel_id=1, source_target_pairs={{0,8},{1,9},{2,10},{3,11},{4,12},{5,13},{6,14},{7,15},{8,0},{9,1},... | collective-permute-start | bytes 4915208 | tf_op jit(solution)/shard_map/ppermute | solution.py:202
  431.2 79.3 %collective-permute-start.48 = (bf16[512,1280]{1,0:T(8,128)(2,1)S(1)}, bf16[512,1280]{1,0:T(8,128)(2,1)S(1)}, u32[]{:S(2)}, u32[]{:S(2)}) collective-permute-start(bf16[512,1280]{1,0:T(8,128)(2,1)S(1)} %get-tuple-element.53), channel_id=1, source_target_pairs={{0,4},{1,5},{2,6},{3,7},{4,0},{5,1},{6,2},{7,3},{8,12},{9,13},{10,... | collective-permute-start | bytes 3932168 | tf_op jit(solution)/shard_map/ppermute | solution.py:202
  433.2 48.4 %collective-permute-start.74 = (bf16[1,2,160,1280]{3,2,1,0:T(8,128)(2,1)S(1)}, bf16[1,2,160,1280]{3,2,1,0:T(8,128)(2,1)S(1)}, u32[]{:S(2)}, u32[]{:S(2)}) collective-permute-start(bf16[1,2,160,1280]{3,2,1,0:T(8,128)(2,1)S(1)} %add_convert_fusion.4), channel_id=1, source_target_pairs={{0,16},{1,17},{2,18},{3,19},{4,20},{5,21},{6,22},{7,23},{8,24},{9,... | collective-permute-start | bytes 2457608 | tf_op jit(solution)/shard_map/ppermute | solution.py:202
  433.9 56.9 %collective-permute-start.77 = (bf16[1,2,160,1280]{3,2,1,0:T(8,128)(2,1)S(1)}, bf16[1,2,160,1280]{3,2,1,0:T(8,128)(2,1)S(1)}, u32[]{:S(2)}, u32[]{:S(2)}) collective-permute-start(bf16[1,2,160,1280]{3,2,1,0:T(8,128)(2,1)S(1)} %add_convert_fusion.3), channel_id=1, source_target_pairs={{0,8},{1,9},{2,10},{3,11},{4,12},{5,13},{6,14},{7,15},{8,0},{9,1},... | collective-permute-start | bytes 2457608 | tf_op jit(solution)/shard_map/ppermute | solution.py:202
  482.9 127.2 %collective-permute-start.75 = (bf16[160,1280]{1,0:T(8,128)(2,1)}, bf16[160,1280]{1,0:T(8,128)(2,1)}, u32[]{:S(2)}, u32[]{:S(2)}) collective-permute-start(bf16[160,1280]{1,0:T(8,128)(2,1)} %get-tuple-element.122), channel_id=1, source_target_pairs={{0,0},{1,1},{6,2},{7,3},{2,4},{3,5},{4,6},{5,7},{8,8},{9,9},{14,10... | collective-permute-start | bytes 1228808 | tf_op jit(solution)/shard_map/ppermute | solution.py:202
  490.9 123.5 %collective-permute-start.79 = (bf16[160,1280]{1,0:T(8,128)(2,1)}, bf16[160,1280]{1,0:T(8,128)(2,1)}, u32[]{:S(2)}, u32[]{:S(2)}) collective-permute-start(bf16[160,1280]{1,0:T(8,128)(2,1)} %get-tuple-element.123), channel_id=1, source_target_pairs={{2,0},{3,1},{4,2},{5,3},{0,4},{1,5},{6,6},{7,7},{10,8},{11,9},{12,... | collective-permute-start | bytes 1228808 | tf_op jit(solution)/shard_map/ppermute | solution.py:202
  499.2 117.4 %collective-permute-start.78 = (bf16[160,1280]{1,0:T(8,128)(2,1)}, bf16[160,1280]{1,0:T(8,128)(2,1)}, u32[]{:S(2)}, u32[]{:S(2)}) collective-permute-start(bf16[160,1280]{1,0:T(8,128)(2,1)} %get-tuple-element.124), channel_id=1, source_target_pairs={{1,0},{0,1},{7,2},{6,3},{3,4},{2,5},{5,6},{4,7},{9,8},{8,9},{15,10... | collective-permute-start | bytes 1228808 | tf_op jit(solution)/shard_map/ppermute | solution.py:202
  507.0 113.8 %collective-permute-start.80 = (bf16[160,1280]{1,0:T(8,128)(2,1)}, bf16[160,1280]{1,0:T(8,128)(2,1)}, u32[]{:S(2)}, u32[]{:S(2)}) collective-permute-start(bf16[160,1280]{1,0:T(8,128)(2,1)} %get-tuple-element.125), channel_id=1, source_target_pairs={{3,0},{2,1},{5,2},{4,3},{1,4},{0,5},{7,6},{6,7},{11,8},{10,9},{13,... | collective-permute-start | bytes 1228808 | tf_op jit(solution)/shard_map/ppermute | solution.py:202
  610.9 110.1 %collective-permute-start.42 = (bf16[256,1280]{1,0:T(8,128)(2,1)S(1)}, bf16[256,1280]{1,0:T(8,128)(2,1)S(1)}, u32[]{:S(2)}, u32[]{:S(2)}) collective-permute-start(bf16[256,1280]{1,0:T(8,128)(2,1)S(1)} %copy-done.67), channel_id=1, source_target_pairs={{1,0},{0,1},{5,2},{4,3},{3,4},{2,5},{7,6},{6,7},{9,8},{8,9},{13,10... | collective-permute-start | bytes 1966088 | tf_op jit(solution)/shard_map/ppermute | solution.py:202
  637.7 83.6 %collective-permute-start.43 = (bf16[256,1280]{1,0:T(8,128)(2,1)S(1)}, bf16[256,1280]{1,0:T(8,128)(2,1)S(1)}, u32[]{:S(2)}, u32[]{:S(2)}) collective-permute-start(bf16[256,1280]{1,0:T(8,128)(2,1)S(1)} %copy-done.66), channel_id=1, source_target_pairs={{0,0},{1,1},{4,2},{5,3},{2,4},{3,5},{6,6},{7,7},{8,8},{9,9},{12,10... | collective-permute-start | bytes 1966088 | tf_op jit(solution)/shard_map/ppermute | solution.py:202
  644.0 73.8 %collective-permute-start.57 = (bf16[2,2,160,1280]{3,2,1,0:T(8,128)(2,1)S(1)}, bf16[2,2,160,1280]{3,2,1,0:T(8,128)(2,1)S(1)}, u32[]{:S(2)}, u32[]{:S(2)}) collective-permute-start(bf16[2,2,160,1280]{3,2,1,0:T(8,128)(2,1)S(1)} %pad_maximum_fusion.4), channel_id=1, source_target_pairs={{0,8},{1,9},{2,10},{3,11},{4,12},{5,13},{6,14},{7,15},{8,0},{9,1},... | collective-permute-start | bytes 4915208 | tf_op jit(solution)/shard_map/ppermute | solution.py:202
  651.4 69.1 %collective-permute-start.60 = (bf16[2,2,160,1280]{3,2,1,0:T(8,128)(2,1)S(1)}, bf16[2,2,160,1280]{3,2,1,0:T(8,128)(2,1)S(1)}, u32[]{:S(2)}, u32[]{:S(2)}) collective-permute-start(bf16[2,2,160,1280]{3,2,1,0:T(8,128)(2,1)S(1)} %pad_maximum_fusion.5), channel_id=1, source_target_pairs={{0,16},{1,17},{2,18},{3,19},{4,20},{5,21},{6,22},{7,23},{8,24},{9,... | collective-permute-start | bytes 4915208 | tf_op jit(solution)/shard_map/ppermute | solution.py:202
  (163 other events, 3516.7 us)

commit v2 on v1

--- a/solution.py
+++ b/solution.py
@@ -271,6 +271,398 @@
     return total
 
 
+MESH = pl.DeviceIdType.MESH
+
+
+class Here:
+    def __init__(self):
+        self.d, self.m = lax.axis_index("dp"), lax.axis_index("mp")
+        self.c = self.d % 2
+        self.pair = self.d - self.c
+        self.x = (self.d // 2) % 2
+        self.y = self.d // 4
+        self.t = self.m // 2
+        self.b = self.m % 2
+        self.over_x = {"dp": self.d + 2 - 4 * self.x, "mp": self.m}
+        self.over_y = {"dp": self.d + 4 - 8 * self.y, "mp": self.m}
+        self.partner = {"dp": self.d + 1 - 2 * self.c, "mp": self.m}
+        self.home = self.t == self.c
+
+    def at(self, core, m):
+        return {"dp": self.pair + core, "mp": m}
+
+
+def remote(src, dst, ssem, rsem, dev):
+    return pltpu.make_async_remote_copy(
+        src_ref=src, dst_ref=dst, send_sem=ssem, recv_sem=rsem, device_id=dev, device_id_type=MESH
+    )
+
+
+def arrived(dst, rsem, dev):
+    remote(dst, dst, rsem, rsem, dev).wait_recv()
+
+
+class Maybe:
+    def __init__(self, src, dst, ssem, rsem, dev, own):
+        self.args, self.dev, self.ssem, self.own = (src, dst), dev, ssem, own
+        self.rsem = rsem
+
+    def far(self):
+        return remote(*self.args, self.ssem, self.rsem, self.dev)
+
+    def start(self):
+        pl.when(self.own)(lambda: pltpu.make_async_copy(*self.args, self.rsem).start())
+        pl.when(jnp.logical_not(self.own))(lambda: self.far().start())
+
+    def wait_send(self):
+        pl.when(jnp.logical_not(self.own))(lambda: self.far().wait_send())
+
+
+def greet(sources, count):
+    barrier = pltpu.get_barrier_semaphore()
+
+    def tell(dev):
+        pl.semaphore_signal(barrier, inc=1, device_id=dev, device_id_type=MESH)
+
+    for dev, own in sources:
+        if own is None:
+            tell(dev)
+        else:
+            pl.when(jnp.logical_not(own))(functools.partial(tell, dev))
+    pl.semaphore_wait(barrier, count)
+
+
+class Gather:
+    def __init__(self, here, shard, full, sems):
+        (self.send_z, self.got_z, self.send_x, self.send_y, self.got_x, self.got_y, self.send_r, self.got_r) = sems
+        self.here, self.shard, self.full = here, shard, full
+        self.rows = shard.shape[0]
+        self.first = jnp.where(here.m > 2 * here.c, 1, 0)
+
+    @staticmethod
+    def scratch():
+        dma = pltpu.SemaphoreType.DMA
+        return [dma((4,)), dma((2, 2))] + [dma((2, 2))] * 6
+
+    def plane(self, i):
+        return (self.first + i) % 2
+
+    def block(self, i, dp):
+        return self.full.at[self.plane(i), pl.ds(dp * self.rows, self.rows), :]
+
+    def z_copy(self, m):
+        h = self.here
+        dst = self.full.at[h.b, pl.ds(h.d * self.rows, self.rows), :]
+        own = jnp.logical_and(h.home, h.m == m)
+        return Maybe(self.shard, dst, self.send_z.at[m], self.got_z.at[h.b, h.c], h.at(h.t, m), own)
+
+    def start_z(self):
+        for m in range(4):
+            self.z_copy(m).start()
+
+    def own_copies(self, i, e):
+        h = self.here
+        ref = self.block(i, h.pair + e)
+        return (
+            remote(ref, ref, self.send_x.at[i, e], self.got_x.at[i, e], h.over_x),
+            remote(ref, ref, self.send_y.at[i, e], self.got_y.at[i, e], h.over_y),
+        )
+
+    def spread(self, i):
+        h = self.here
+        for e in range(2):
+            arrived(self.block(i, h.pair + e), self.got_z.at[self.plane(i), e], h.partner)
+            for copy in self.own_copies(i, e):
+                copy.start()
+
+    def relay_copy(self, i, e):
+        h = self.here
+        if i == 0:
+            ref, dev = self.block(i, h.over_y["dp"] - h.c + e), h.over_x
+        else:
+            ref, dev = self.block(i, h.over_x["dp"] - h.c + e), h.over_y
+        return remote(ref, ref, self.send_r.at[i, e], self.got_r.at[i, e], dev)
+
+    def relay(self, i):
+        h = self.here
+        for e in range(2):
+            if i == 0:
+                arrived(self.block(i, h.over_y["dp"] - h.c + e), self.got_y.at[i, e], h.over_y)
+            else:
+                arrived(self.block(i, h.over_x["dp"] - h.c + e), self.got_x.at[i, e], h.over_x)
+            self.relay_copy(i, e).start()
+
+    def finish(self):
+        h = self.here
+        diagonal = h.pair + 2 - 4 * h.x + 4 - 8 * h.y
+        for i in range(2):
+            for e in range(2):
+                if i == 0:
+                    arrived(self.block(i, h.over_x["dp"] - h.c + e), self.got_x.at[i, e], h.over_x)
+                else:
+                    arrived(self.block(i, h.over_y["dp"] - h.c + e), self.got_y.at[i, e], h.over_y)
+                arrived(self.block(i, diagonal + e), self.got_r.at[i, e], h.over_x)
+        for m in range(4):
+            self.z_copy(m).wait_send()
+        for i in range(2):
+            for e in range(2):
+                for copy in self.own_copies(i, e):
+                    copy.wait_send()
+                self.relay_copy(i, e).wait_send()
+
+
+class ToCell:
+    def __init__(self, here, source, rows, send, got):
+        self.here, self.source, self.rows, self.send, self.got = here, source, rows, send, got
+
+    def copy(self, s):
+        h = self.here
+        target = 2 * h.c + s
+        own = jnp.logical_and(h.home, h.m == target)
+        return Maybe(self.source.at[s], self.rows.at[h.b], self.send.at[s], self.got.at[h.b], h.at(h.t, target), own)
+
+    def start(self):
+        for s in range(2):
+            self.copy(s).start()
+
+    def wait(self):
+        for b in range(2):
+            arrived(self.rows.at[b], self.got.at[b], self.here.partner)
+
+    def finish(self):
+        for s in range(2):
+            self.copy(s).wait_send()
+
+
+def spread_ends(here):
+    h = here
+    takers = [(h.at(h.t, m), jnp.logical_and(h.home, h.m == m)) for m in range(4)]
+    givers = [(h.at(e, 2 * h.c + b), jnp.logical_and(h.home, jnp.logical_and(h.b == b, h.c == e))) for e in range(2) for b in range(2)]
+    return takers, givers
+
+
+def greet_cross(here, sources, *others):
+    others = [here.over_x, here.over_y, *others]
+    greet(sources + [(dev, None) for dev in others], 4 + len(others) - here.home.astype(jnp.int32))
+
+
+def norm_rows(values, gain, shift):
+    mean_row = jnp.mean(values, axis=-1, keepdims=True)
+    centred = values - mean_row
+    inv_std = lax.rsqrt(jnp.mean(centred * centred, axis=-1, keepdims=True) + eps_norm)
+    return centred * inv_std * gain + shift
+
+
+def gather_first_kernel(x_ref, shard_ref, norm_ref, full_ref, h_ref, x_out, *sems):
+    here = Here()
+    send_x, got_x, send_h, got_h = sems[:4]
+    greet_cross(here, spread_ends(here)[1], here.partner)
+    block = Gather(here, shard_ref, full_ref, sems[4:])
+    cell = ToCell(here, x_ref, x_out, send_x, got_x)
+    block.start_z()
+    cell.start()
+    block.spread(0)
+    block.spread(1)
+    cell.wait()
+    quarter = x_out.shape[1]
+    for b in range(2):
+        h_ref[0, pl.ds(b * quarter, quarter), :] = norm_rows(
+            x_out[b].astype(F32), norm_ref[0:1, :], norm_ref[1:2, :]
+        ).astype(BF16)
+    swap = remote(h_ref.at[0], h_ref.at[1], send_h, got_h, here.partner)
+    swap.start()
+    block.relay(0)
+    block.relay(1)
+    block.finish()
+    cell.finish()
+    swap.wait()
+
+
+ANY = pl.BlockSpec(memory_space=pl.ANY)
+VMEM = pl.BlockSpec(memory_space=pltpu.VMEM)
+
+
+def gather_first(inputs, shard, norms, collective):
+    cells, quarter, width = inputs.shape
+    rows = shard.shape[0]
+    dma = pltpu.SemaphoreType.DMA
+    return pl.pallas_call(
+        gather_first_kernel,
+        out_shape=[
+            jax.ShapeDtypeStruct((2, 8 * rows, width), BF16),
+            jax.ShapeDtypeStruct((2, 2 * quarter, width), BF16),
+            jax.ShapeDtypeStruct((2, quarter, width), BF16),
+        ],
+        in_specs=[VMEM, VMEM, VMEM],
+        out_specs=[ANY, VMEM, VMEM],
+        scratch_shapes=[dma((2,)), dma((2,)), dma, dma] + Gather.scratch(),
+        compiler_params=pltpu.CompilerParams(collective_id=collective, has_side_effects=True),
+        name="gather_first",
+    )(inputs, shard, norms)
+
+
+def gather_rest_kernel(gy_ref, shard_one, shard_two, full_one, full_two, gy_out, *sems):
+    here = Here()
+    send_g, got_g = sems[:2]
+    greet_cross(here, spread_ends(here)[1])
+    blocks = [Gather(here, shard_one, full_one, sems[2:10]), Gather(here, shard_two, full_two, sems[10:18])]
+    cell = ToCell(here, gy_ref, gy_out, send_g, got_g)
+    for block in blocks:
+        block.start_z()
+    cell.start()
+    for block in blocks:
+        block.spread(0)
+        block.spread(1)
+        block.relay(0)
+        block.relay(1)
+    for block in blocks:
+        block.finish()
+    cell.wait()
+    cell.finish()
+
+
+def gather_rest(cotangent, shard_one, shard_two, collective):
+    cells, quarter, width = cotangent.shape
+    rows = shard_one.shape[0]
+    dma = pltpu.SemaphoreType.DMA
+    return pl.pallas_call(
+        gather_rest_kernel,
+        out_shape=[jax.ShapeDtypeStruct((2, 8 * rows, width), BF16)] * 2
+        + [jax.ShapeDtypeStruct((2, quarter, width), BF16)],
+        in_specs=[VMEM] * 3,
+        out_specs=[ANY] * 3,
+        scratch_shapes=[dma((2,)), dma((2,))] + Gather.scratch() * 2,
+        compiler_params=pltpu.CompilerParams(collective_id=collective, has_side_effects=True),
+        name="gather_rest",
+    )(cotangent, shard_one, shard_two)
+
+
+class Reduce:
+    def __init__(self, here, grads, bufs, sems):
+        self.here, self.grads = here, grads
+        self.own, self.one, self.two, self.part, self.last = bufs
+        self.sem_own, self.send_one, self.got_one, self.send_two, self.got_two, self.send_z, self.got_z = sems
+        self.piece = self.own.shape[3]
+
+    @staticmethod
+    def scratch(rows, width):
+        r = rows // 2
+        dma = pltpu.SemaphoreType.DMA
+        return [
+            pltpu.VMEM((2, 2, 4, r, width), BF16),
+            pltpu.VMEM((2, 2, 4, r, width), BF16),
+            pltpu.VMEM((2, 4, r, width), BF16),
+            pltpu.VMEM((2, 4, r, width), BF16),
+            pltpu.VMEM((4, 2, r, width), BF16),
+        ], [dma((2, 2, 4)), dma((2, 2, 4)), dma((2, 2, 4)), dma((2, 4)), dma((2, 4)), dma((2, 4)), dma((4, 2))]
+
+    def rows_of(self, role, dp, j):
+        return self.grads.at[role, pl.ds(dp * 2 * self.piece + j * self.piece, self.piece), :]
+
+    def pair_at(self, role, n, far):
+        h = self.here
+        dx, dy = 2 - 4 * h.x, 4 - 8 * h.y
+        first, second = (dx, dy) if role == 0 else (dy, dx)
+        return h.pair + (first if far else 0) + (second if n == 0 else 0)
+
+    def load(self, role, n, j):
+        return pltpu.make_async_copy(
+            self.rows_of(role, self.pair_at(role, n, False), j), self.own.at[role, n, j], self.sem_own.at[role, n, j]
+        )
+
+    def copy_one(self, role, n, j):
+        dev = self.here.over_x if role == 0 else self.here.over_y
+        return remote(
+            self.rows_of(role, self.pair_at(role, n, True), j), self.one.at[role, n, j],
+            self.send_one.at[role, n, j], self.got_one.at[role, n, j], dev,
+        )
+
+    def copy_two(self, role, j):
+        dev = self.here.over_y if role == 0 else self.here.over_x
+        return remote(
+            self.own.at[role, 0, j], self.two.at[role, j], self.send_two.at[role, j], self.got_two.at[role, j], dev
+        )
+
+    def copy_z(self, role, j):
+        h = self.here
+        core, target = j // 2, 2 * h.c + role
+        own = jnp.logical_and(h.c == core, h.m == target)
+        return Maybe(
+            self.part.at[role, j], self.last.at[h.m, j % 2], self.send_z.at[role, j], self.got_z.at[h.m, j % 2],
+            h.at(core, target), own,
+        )
+
+    def start(self):
+        for j in range(4):
+            for n in range(2):
+                for role in range(2):
+                    self.copy_one(role, n, j).start()
+                    self.load(role, n, j).start()
+
+    def add_one(self, role, j):
+        h = self.here
+        for n in range(2):
+            self.load(role, n, j).wait()
+            arrived(self.one.at[role, n, j], self.got_one.at[role, n, j], h.over_x)
+            total = self.own[role, n, j].astype(F32) + self.one[role, n, j].astype(F32)
+            self.own[role, n, j] = total.astype(BF16)
+            if n == 0:
+                self.copy_two(role, j).start()
+
+    def add_two(self, role, j):
+        arrived(self.two.at[role, j], self.got_two.at[role, j], self.here.over_x)
+        total = self.own[role, 1, j].astype(F32) + self.two[role, j].astype(F32)
+        self.part[role, j] = total.astype(BF16)
+        self.copy_z(role, j).start()
+
+    def finish(self, out_ref):
+        h = self.here
+        for s in range(2):
+            for m in range(4):
+                arrived(self.last.at[m, s], self.got_z.at[m, s], h.partner)
+            total = self.last[0, s].astype(F32)
+            for m in range(1, 4):
+                total = total + self.last[m, s].astype(F32)
+            out_ref[pl.ds(s * self.piece, self.piece), :] = total
+        for role in range(2):
+            for j in range(4):
+                for n in range(2):
+                    self.copy_one(role, n, j).wait_send()
+                self.copy_two(role, j).wait_send()
+                self.copy_z(role, j).wait_send()
+
+
+def reduce_kernel(grads_ref, out_ref, *scratch):
+    here = Here()
+    greet_cross(here, spread_ends(here)[0])
+    block = Reduce(here, grads_ref, scratch[:5], scratch[5:])
+    block.start()
+    for j in range(4):
+        for role in range(2):
+            block.add_one(role, j)
+        if j >= 1:
+            for role in range(2):
+                block.add_two(role, j - 1)
+    for role in range(2):
+        block.add_two(role, 3)
+    block.finish(out_ref)
+
+
+def reduce_block(grads, collective):
+    _, full, width = grads.shape
+    rows = full // 8
+    bufs, sems = Reduce.scratch(rows, width)
+    return pl.pallas_call(
+        reduce_kernel,
+        out_shape=jax.ShapeDtypeStruct((rows, width), F32),
+        in_specs=[ANY],
+        out_specs=VMEM,
+        scratch_shapes=bufs + sems,
+        compiler_params=pltpu.CompilerParams(collective_id=collective, has_side_effects=True),
+        name="reduce_block",
+    )(grads)
+
+
 def gather_norms(routes, norm_params, d, m):
     cur = norm_params
     for bit in range(routes.mp_bits):
@@ -326,6 +718,9 @@
 
     def from_cell(rows):
         rows = rows.astype(BF16)
+        if kernels:
+            flip_rows = jnp.concatenate([rows[quarter:], rows[:quarter]], 0)
+            rows = jnp.where(m_low == 1, flip_rows, rows)
         got = [routes.cell(rows[k * quarter : (k + 1) * quarter], k, back=True) for k in range(2)]
         flip = m_low == 1
         return jnp.stack([jnp.where(flip, got[1], got[0]), jnp.where(flip, got[0], got[1])]).astype(F32)
@@ -336,21 +731,26 @@
     expand_shard = expand_weight.astype(BF16)
     reduce_shard = reduce_weight.T.astype(BF16)
 
-    x_mine = to_cell(inputs).astype(F32)
-    attend_w = [assemble(pieces, mask) for pieces in gather_shards(routes, attend_shard)]
-    expand_w = [assemble(pieces, mask) for pieces in gather_shards(routes, expand_shard)]
-    reduce_w = [assemble(pieces, mask) for pieces in gather_shards(routes, reduce_shard)]
-    gy_mine = to_cell(cotangent)
+    kernels = routes.dp == 8 and routes.mp == 4
+    if kernels:
+        attend_w, h1, x_mine = gather_first(inputs, attend_shard, norm_full[0:2], 1)
+        x_mine = x_mine.reshape(half, -1).astype(F32)
+        expand_w, reduce_w, gy_mine = gather_rest(cotangent, expand_shard, reduce_shard, 2)
+        gy_mine = gy_mine.reshape(half, -1)
+    else:
+        x_mine = to_cell(inputs).astype(F32)
+        attend_w = [assemble(pieces, mask) for pieces in gather_shards(routes, attend_shard)]
+        expand_w = [assemble(pieces, mask) for pieces in gather_shards(routes, expand_shard)]
+        reduce_w = [assemble(pieces, mask) for pieces in gather_shards(routes, reduce_shard)]
+        gy_mine = to_cell(cotangent)
 
     other_counts = routes.partner(gene_counts)
     mine = jnp.where(m_high == c, gene_counts, other_counts)
     count = jnp.where(m_low == 1, mine[1], mine[0])
     inside = jnp.arange(quarter)
+    first = 0 if kernels else m_low
     positions = jnp.concatenate(
-        [
-            h * half + b * quarter + inside
-            for h, b in ((c, m_low), (c, 1 - m_low), (1 - c, m_low), (1 - c, 1 - m_low))
-        ]
+        [h * half + b * quarter + inside for h, b in ((c, first), (c, 1 - first), (1 - c, first), (1 - c, 1 - first))]
     )
     bias = jnp.where(positions < 1 + count, 0.0, masked_score).astype(F32)
 
@@ -361,7 +761,7 @@
         return partial[:half] + routes.partner(partial[half:].astype(BF16)).astype(F32)
 
     normed, scaled_one, inv_one = normalize(x_mine, norm_full[0], norm_full[1])
-    h1 = both(normed.astype(BF16))
+    h1 = h1.reshape(seq, -1) if kernels else both(normed.astype(BF16))
     qkv = jnp.stack([mm_nn(h1, w[:, : 3 * width]).astype(BF16) for w in attend_w])
     ctx, lse = attend(qkv, bias[None, :], heads)
     branch = mm_nt(ctx[0], attend_w[0][:, 3 * width :]) + mm_nt(ctx[1], attend_w[1][:, 3 * width :])
@@ -400,9 +800,14 @@
     grad_in, gain_one, shift_one = normalize_back(gh1, scaled_one, inv_one, norm_full[0])
     input_grad = from_cell(gx2 + grad_in)
 
-    reduce_sum = scatter_grads(routes, reduce_grad, mask)
-    expand_sum = scatter_grads(routes, expand_grad, mask)
-    attend_sum = scatter_grads(routes, attend_grad, mask)
+    if kernels:
+        reduce_sum = reduce_block(jnp.stack(reduce_grad), 3)
+        expand_sum = reduce_block(jnp.stack(expand_grad), 3)
+        attend_sum = reduce_block(jnp.stack(attend_grad), 3)
+    else:
+        reduce_sum = scatter_grads(routes, reduce_grad, mask)
+        expand_sum = scatter_grads(routes, expand_grad, mask)
+        attend_sum = scatter_grads(routes, attend_grad, mask)
     norm_sum = scatter_norms(routes, jnp.stack([gain_one, shift_one, gain_two, shift_two]), d, m)
 
     step_number = step_count[0].astype(F32)

time: 799 us -> 820 us (1.026)
  Pallas kernels: 60.6 us -> 523 us
  waiting for transfers between devices: 287 us -> 27.9 us
  starting transfers between devices: 173 us -> 31.7 us
  local copies, waits for them, and re-layouts: 85.4 us -> 32.9 us
  matrix products: 127 us -> 136 us
    pallas_call x0 -> x5, Pallas kernels: none -> 462 us  [the longest x3 247 us: reduce_block(): pl.pallas_call(reduce_kernel, out_shape=jax.ShapeDtypeStruct((rows, width...]
    ppermute x81 -> x22, waiting for transfers between devices: 287 us -> 27.9 us  [send(): return lax.ppermute(value, AXES, pairs)]
    ppermute x81 -> x22, starting transfers between devices: 173 us -> 31.7 us  [send(): return lax.ppermute(value, AXES, pairs)]
    dynamic_update_slice x48 -> x0, local copies, waits for them, and re-layouts: 23.7 us -> none  [assemble(): lax.dynamic_update_slice(full, pieces[r][e], ((2 * r + e ^ mask) * rows, 0))]
    unnamed x213 -> x134, local copies, waits for them, and re-layouts: 17.5 us -> 5.99 us
    dot_general x28, matrix products: 127 us -> 136 us  [mm(): lax.dot_general(left, right, (dims, ((), ())), preferred_element_type=F32)]
    another operation x25 -> x4, other arithmetic: 4.75 us -> 13.1 us  [the longest x1 5.29 us: per_device(): attend_sum = reduce_block(jnp.stack(attend_grad), 3)]
  transfers between devices with their start and end apart: 81 -> 22, of which waited for: 39 -> 8; matrix products, arithmetic and copies ran while one was open for 23% -> 18% of each run, Pallas kernels for 8% -> 52%
where the time goes in v2:
time: 820 us; the launch traced here: 806 us
  Pallas kernels  523 us (64%)
  matrix products  136 us (17%)
  other arithmetic  51.6 us (6%)
  local copies, waits for them, and re-layouts  32.9 us (4%)
  starting transfers between devices  31.7 us (4%)
  waiting for transfers between devices  27.9 us (3%)
    pallas_call x3, Pallas kernels, reduce_block(): pl.pallas_call(reduce_kernel, out_shape=jax.ShapeDtypeStruct((rows, width...  247 us
    pallas_call x1, Pallas kernels, gather_rest(): pl.pallas_call(gather_rest_kernel, out_shape=[jax.ShapeDtypeStruct((2, 8...  138 us
    dot_general x28, matrix products, mm(): lax.dot_general(left, right, (dims, ((), ())), preferred_element_type=F32)  136 us
    pallas_call x1, Pallas kernels, gather_first(): pl.pallas_call(gather_first_kernel, out_shape=[jax.ShapeDtypeStruct((2, 8...  77.5 us
    pallas_call x1, Pallas kernels, attend_back(): pl.pallas_call(functools.partial(attend_back_kernel, heads), grid=(chunks...  35.1 us
    ppermute x22, starting transfers between devices, send(): return lax.ppermute(value, AXES, pairs)  31.7 us
    ppermute x22, waiting for transfers between devices, send(): return lax.ppermute(value, AXES, pairs)  27.9 us
    pallas_call x1, Pallas kernels, attend(): pl.pallas_call(functools.partial(attend_kernel, heads, block), grid=(chun...  25.4 us
  transfers between devices with their start and end apart: 22, of which 8 were waited for; matrix products, arithmetic and copies ran while one was open for 18% of the time, Pallas kernels for 52%

profile of v2, /device:TPU:1, one launch (start us, length us, event | category | flops | bytes accessed | tf_op | source)
XLA Modules:
  0.0 806.2 jit_solution(4323167920061357717)
XLA Ops:
  18.7 77.5 %gather_first.1 = (bf16[2,1280,1280]{2,1,0:T(8,128)(2,1)}, bf16[2,512,1280]{2,1,0:T(8,128)(2,1)}, bf16[2,256,1280]{2,1,0:T(8,128)(2,1)}) custom-call(bf16[2,256,1280]{2,1,0:T(8,128)(2,1)} %x_ref.1, bf16[160,1280]{1,0:T(8,128)(2,1)} %concatenate.118.shard_ref, f32[2,1280]{1,0:T(2,128)} %slice.215.norm_ref), custom_call_target="tpu_custom_call" | custom-call | tf_op jit(solution)/shard_map/gather_first/pallas_call | solution.py:489
  108.4 25.4 %attend.1 = (bf16[2,1024,320]{2,1,0:T(8,128)(2,1)}, f32[2,1024,8]{2,1,0:T(8,128)}) custom-call(f32[1,1024]{1,0:T(1,128)} %compare_select_fusion.bias_ref, bf16[2,1024,960]{2,1,0:T(8,128)(2,1)} %pad_maximum_fusion.3.q_ref.kv_ref, bf16[2,1024,960]{2,1,0:T(8,128)(2,1)} %pad_maximum_fusion.3.q_ref.kv_ref), custom_call_target="tpu_custom_call" | custom-call | flops 10737418240 | bytes 5242880 | tf_op jit(solution)/shard_map/attend/pallas_call | solution.py:94
  145.8 137.5 %gather_rest.1 = (bf16[2,1280,1280]{2,1,0:T(8,128)(2,1)}, bf16[2,1280,1280]{2,1,0:T(8,128)(2,1)}, bf16[2,256,1280]{2,1,0:T(8,128)(2,1)}) custom-call(bf16[2,256,1280]{2,1,0:T(8,128)(2,1)} %gy_ref.1, bf16[160,1280]{1,0:T(8,128)(2,1)} %convert_element_type.118.shard_one, bf16[160,1280]{1,0:T(8,128)(2,1)} %convert_bitcast_fusion.2.shard_two), custom_call_target="tpu_custom_call" | custom-call | tf_op jit(solution)/shard_map/gather_rest/pallas_call | solution.py:528
  287.3 19.1 %multiply_convert_fusion.1 = (bf16[1024,1280]{1,0:T(8,128)(2,1)}, f32[1024,1280]{1,0:T(8,128)S(1)}, f32[1024,1280]{1,0:T(8,128)}) fusion(bf16[2,1280,1280]{2,1,0:T(8,128)(2,1)} %get-tuple-element.32, bf16[512,1280]{1,0:T(8,128)(2,1)} %collective-permute-done.7, bf16[512,1280]{1,0:T(8,128)(2,1)S(1)} %add_convert_fusion.2), kind=kOutput, calls=%fused_computation.31 | convolution fusion | flops 3445882880 | bytes 19005440 | tf_op jit(solution)/shard_map/dot_general | solution.py:33
  306.5 7.4 add_convert_fusion.1
  317.6 17.6 %multiply_convert_fusion = (bf16[1024,1280]{1,0:T(8,128)(2,1)}, f32[1024,1280]{1,0:T(8,128)}, f32[1024,1280]{1,0:T(8,128)}) fusion(bf16[2,1280,1280]{2,1,0:T(8,128)(2,1)S(1)} %bitcast.212, bf16[512,1280]{1,0:T(8,128)(2,1)} %collective-permute-done.7, bf16[512,1280]{1,0:T(8,128)(2,1)S(1)} %add_convert_fusion.2), kind=kOutput, calls=%fused_computation.18 | convolution fusion | flops 3445882880 | bytes 19005440 | tf_op jit(solution)/shard_map/dot_general | solution.py:33
  335.2 8.3 %add_convert_fusion = bf16[1024,1280]{1,0:T(8,128)(2,1)S(1)} fusion(f32[1024,1280]{1,0:T(8,128)} %get-tuple-element.67, f32[1024,1280]{1,0:T(8,128)} %get-tuple-element.100, bf16[2,1280,1280]{2,1,0:T(8,128)(2,1)S(1)} %bitcast.210, bf16[512,1280]{1,0:T(8,128)(2,1)} %collective-permute-done.11, bf16[512,1280]{1,0:T(8,128)(2,1)S(1)} %bitcast.195), kind=kOutput, calls=%fused_computation.16 | convolution fusion | flops 3379036160 | bytes 19005440 | tf_op jit(solution)/shard_map/dot_general | solution.py:33
  348.9 5.7 fusion.26
  360.2 6.1 fusion.1
  366.3 5.4 fusion
  375.1 75.8 %reduce_block.4 = f32[160,1280]{1,0:T(8,128)} custom-call(bf16[2,1280,1280]{2,1,0:T(8,128)(2,1)} %pad_maximum_fusion.1.grads_ref), custom_call_target="tpu_custom_call" | custom-call | tf_op jit(solution)/shard_map/reduce_block/pallas_call | solution.py:655
  450.9 6.3 fusion.3
  457.2 5.0 fusion.2
  465.4 89.2 %reduce_block.5 = f32[160,1280]{1,0:T(8,128)} custom-call(bf16[2,1280,1280]{2,1,0:T(8,128)(2,1)} %pad_maximum_fusion.2.grads_ref), custom_call_target="tpu_custom_call" | custom-call | tf_op jit(solution)/shard_map/reduce_block/pallas_call | solution.py:655
  562.7 4.2 fusion.126
  568.5 5.4 collective-permute-start.10
  583.1 35.1 %attend_back.1 = (bf16[2,1024,320]{2,1,0:T(8,128)(2,1)}, bf16[2,1024,640]{2,1,0:T(8,128)(2,1)}) custom-call(f32[1024,1]{1,0:T(8,128)} %broadcast_select_fusion.bias_ref, bf16[2,1024,960]{2,1,0:T(8,128)(2,1)} %pad_maximum_fusion.3.q_ref.kv_ref, bf16[2,1024,320]{2,1,0:T(8,128)(2,1)} %pad_maximum_fusion.7.g_ref, bf16[2,1024,320]{2,1,0:T(8,128)(2,1)} %get-tuple-element.31.o_ref, ...), custom_call_target="tpu_custom_call" | custom-call | flops 26843545600 | bytes 13107200 | tf_op jit(solution)/shard_map/attend_back/pallas_call | solution.py:155
  648.4 5.9 concatenate.151
  654.3 4.4 fusion.64
  658.7 7.0 concatenate.147
  665.7 5.3 pad_maximum_fusion.grads_ref
  671.0 82.0 %reduce_block.3 = f32[160,1280]{1,0:T(8,128)} custom-call(bf16[2,1280,1280]{2,1,0:T(8,128)(2,1)} %pad_maximum_fusion.grads_ref), custom_call_target="tpu_custom_call" | custom-call | tf_op jit(solution)/shard_map/reduce_block/pallas_call | solution.py:655
  778.8 14.5 %collective-permute-done.21 = f32[4,40]{1,0:T(4,128)S(1)} collective-permute-done((f32[4,40]{1,0:T(4,128)S(1)}, f32[4,40]{1,0:T(4,128)S(1)}, u32[]{:S(2)}, u32[]{:S(2)}) %collective-permute-start.21) | collective-permute-done | bytes 672 | tf_op jit(solution)/shard_map/ppermute | solution.py:202
  794.6 6.7 collective-permute-done.16
  (275 shorter events, 145.3 us)
Async XLA Ops:
  0.7 5.4 collective-permute-start
  2.8 8.6 %collective-permute-start.5 = (s32[2]{0:T(128)}, s32[2]{0:T(128)S(1)}, u32[]{:S(2)}, u32[]{:S(2)}) collective-permute-start(s32[2]{0:T(128)} %param.21), channel_id=1, source_target_pairs={{0,4},{1,5},{2,6},{3,7},{4,0},{5,1},{6,2},{7,3},{8,12},{9,13},{10,... | collective-permute-start | bytes 32 | tf_op jit(solution)/shard_map/ppermute | solution.py:202
  6.9 3.3 collective-permute-start.1
  10.3 2.0 collective-permute-start.2
  12.3 3.1 collective-permute-start.3
  15.5 2.5 collective-permute-start.4
  138.8 3.1 collective-permute-start.6
  143.9 173.7 %copy-start.26 = (bf16[512,1280]{1,0:T(8,128)(2,1)}, bf16[512,1280]{1,0:T(8,128)(2,1)S(1)}, u32[]{:S(2)}) copy-start(bf16[512,1280]{1,0:T(8,128)(2,1)S(1)} %add_convert_fusion.2) | copy-start | bytes 3932164
  143.9 143.4 %collective-permute-start.7 = (bf16[512,1280]{1,0:T(8,128)(2,1)S(1)}, bf16[512,1280]{1,0:T(8,128)(2,1)}, u32[]{:S(2)}, u32[]{:S(2)}) collective-permute-start(bf16[512,1280]{1,0:T(8,128)(2,1)S(1)} %add_convert_fusion.2), channel_id=1, source_target_pairs={{0,4},{1,5},{2,6},{3,7},{4,0},{5,1},{6,2},{7,3},{8,12},{9,13},{10,... | collective-permute-start | bytes 3932168 | tf_op jit(solution)/shard_map/ppermute | solution.py:202
  283.4 23.1 %collective-permute-start.11 = (bf16[512,1280]{1,0:T(8,128)(2,1)}, bf16[512,1280]{1,0:T(8,128)(2,1)}, u32[]{:S(2)}, u32[]{:S(2)}) collective-permute-start(bf16[512,1280]{1,0:T(8,128)(2,1)} %bitcast.192), channel_id=1, source_target_pairs={{0,4},{1,5},{2,6},{3,7},{4,0},{5,1},{6,2},{7,3},{8,12},{9,13},{10,... | collective-permute-start | bytes 3932168 | tf_op jit(solution)/shard_map/ppermute | solution.py:202
  348.5 211.8 %collective-permute-start.12 = (bf16[512,1280]{1,0:T(8,128)(2,1)}, bf16[512,1280]{1,0:T(8,128)(2,1)S(1)}, u32[]{:S(2)}, u32[]{:S(2)}) collective-permute-start(bf16[512,1280]{1,0:T(8,128)(2,1)} %slice.377), channel_id=1, source_target_pairs={{0,4},{1,5},{2,6},{3,7},{4,0},{5,1},{6,2},{7,3},{8,12},{9,13},{10,... | collective-permute-start | bytes 3932168 | tf_op jit(solution)/shard_map/ppermute | solution.py:202
  359.7 203.0 %collective-permute-start.8 = (bf16[512,1280]{1,0:T(8,128)(2,1)}, bf16[512,1280]{1,0:T(8,128)(2,1)}, u32[]{:S(2)}, u32[]{:S(2)}) collective-permute-start(bf16[512,1280]{1,0:T(8,128)(2,1)} %slice.378), channel_id=1, source_target_pairs={{0,4},{1,5},{2,6},{3,7},{4,0},{5,1},{6,2},{7,3},{8,12},{9,13},{10,... | collective-permute-start | bytes 3932168 | tf_op jit(solution)/shard_map/ppermute | solution.py:202
  465.4 94.8 %slice-start.2 = ((s8[5242880]{0:T(1024)(128)(4,1)}), s8[1048576]{0:T(1024)(128)(4,1)S(1)}, s32[]{:S(2)}) async-start(s8[5242880]{0:T(1024)(128)(4,1)} %bitcast.190), calls=%async_computation.2 | async-start | bytes 2097152
  566.9 10.3 %collective-permute-start.13 = (bf16[512,1280]{1,0:T(8,128)(2,1)S(1)}, bf16[512,1280]{1,0:T(8,128)(2,1)S(1)}, u32[]{:S(2)}, u32[]{:S(2)}) collective-permute-start(bf16[512,1280]{1,0:T(8,128)(2,1)S(1)} %get-tuple-element.64), channel_id=1, source_target_pairs={{0,4},{1,5},{2,6},{3,7},{4,0},{5,1},{6,2},{7,3},{8,12},{9,13},{10,... | collective-permute-start | bytes 3932168 | tf_op jit(solution)/shard_map/ppermute | solution.py:202
  568.5 226.0 %collective-permute-start.10 = (bf16[256,1280]{1,0:T(8,128)(2,1)}, bf16[256,1280]{1,0:T(8,128)(2,1)}, u32[]{:S(2)}, u32[]{:S(2)}) collective-permute-start(bf16[256,1280]{1,0:T(8,128)(2,1)} %get-tuple-element.84), channel_id=1, source_target_pairs={{0,0},{1,1},{4,2},{5,3},{2,4},{3,5},{6,6},{7,7},{8,8},{9,9},{12,10... | collective-permute-start | bytes 1966088 | tf_op jit(solution)/shard_map/ppermute | solution.py:202
  574.0 220.6 %collective-permute-start.9 = (bf16[256,1280]{1,0:T(8,128)(2,1)}, bf16[256,1280]{1,0:T(8,128)(2,1)}, u32[]{:S(2)}, u32[]{:S(2)}) collective-permute-start(bf16[256,1280]{1,0:T(8,128)(2,1)} %get-tuple-element.83), channel_id=1, source_target_pairs={{1,0},{0,1},{5,2},{4,3},{3,4},{2,5},{7,6},{6,7},{9,8},{8,9},{13,10... | collective-permute-start | bytes 1966088 | tf_op jit(solution)/shard_map/ppermute | solution.py:202
  643.6 112.7 %collective-permute-start.14 = (bf16[512,1280]{1,0:T(8,128)(2,1)}, bf16[512,1280]{1,0:T(8,128)(2,1)}, u32[]{:S(2)}, u32[]{:S(2)}) collective-permute-start(bf16[512,1280]{1,0:T(8,128)(2,1)} %slice.376), channel_id=1, source_target_pairs={{0,4},{1,5},{2,6},{3,7},{4,0},{5,1},{6,2},{7,3},{8,12},{9,13},{10,... | collective-permute-start | bytes 3932168 | tf_op jit(solution)/shard_map/ppermute | solution.py:202
  760.0 3.5 collective-permute-start.17
  763.7 2.5 collective-permute-start.18
  766.3 1.2 collective-permute-start.19
  767.6 7.0 collective-permute-start.20
  770.8 23.8 %collective-permute-start.15 = (bf16[256,1280]{1,0:T(8,128)(2,1)S(1)}, bf16[256,1280]{1,0:T(8,128)(2,1)S(1)}, u32[]{:S(2)}, u32[]{:S(2)}) collective-permute-start(bf16[256,1280]{1,0:T(8,128)(2,1)S(1)} %get-tuple-element.77), channel_id=1, source_target_pairs={{1,0},{0,1},{5,2},{4,3},{3,4},{2,5},{7,6},{6,7},{9,8},{8,9},{13,10... | collective-permute-start | bytes 1966088 | tf_op jit(solution)/shard_map/ppermute | solution.py:202
  772.7 28.6 %collective-permute-start.16 = (bf16[256,1280]{1,0:T(8,128)(2,1)S(1)}, bf16[256,1280]{1,0:T(8,128)(2,1)S(1)}, u32[]{:S(2)}, u32[]{:S(2)}) collective-permute-start(bf16[256,1280]{1,0:T(8,128)(2,1)S(1)} %get-tuple-element.78), channel_id=1, source_target_pairs={{0,0},{1,1},{4,2},{5,3},{2,4},{3,5},{6,6},{7,7},{8,8},{9,9},{12,10... | collective-permute-start | bytes 1966088 | tf_op jit(solution)/shard_map/ppermute | solution.py:202
  774.7 18.5 %collective-permute-start.21 = (f32[4,40]{1,0:T(4,128)S(1)}, f32[4,40]{1,0:T(4,128)S(1)}, u32[]{:S(2)}, u32[]{:S(2)}) collective-permute-start(f32[4,40]{1,0:T(4,128)S(1)} %slice_select_fusion.4), channel_id=1, source_target_pairs={{0,1},{1,0},{2,3},{3,2},{4,5},{5,4},{6,7},{7,6},{8,9},{9,8},{10,11... | collective-permute-start | bytes 1928 | tf_op jit(solution)/shard_map/ppermute | solution.py:202
  (64 other events, 817.5 us)

commit v3 on v2

--- a/solution.py
+++ b/solution.py
@@ -393,6 +393,10 @@
             self.relay_copy(i, e).start()
 
     def finish(self):
+        self.arrive()
+        self.sent()
+
+    def arrive(self):
         h = self.here
         diagonal = h.pair + 2 - 4 * h.x + 4 - 8 * h.y
         for i in range(2):
@@ -402,6 +406,8 @@
                 else:
                     arrived(self.block(i, h.over_y["dp"] - h.c + e), self.got_y.at[i, e], h.over_y)
                 arrived(self.block(i, diagonal + e), self.got_r.at[i, e], h.over_x)
+
+    def sent(self):
         for m in range(4):
             self.z_copy(m).wait_send()
         for i in range(2):
@@ -453,88 +459,261 @@
     return centred * inv_std * gain + shift
 
 
-def gather_first_kernel(x_ref, shard_ref, norm_ref, full_ref, h_ref, x_out, *sems):
-    here = Here()
-    send_x, got_x, send_h, got_h = sems[:4]
-    greet_cross(here, spread_ends(here)[1], here.partner)
-    block = Gather(here, shard_ref, full_ref, sems[4:])
-    cell = ToCell(here, x_ref, x_out, send_x, got_x)
-    block.start_z()
-    cell.start()
-    block.spread(0)
-    block.spread(1)
-    cell.wait()
-    quarter = x_out.shape[1]
-    for b in range(2):
-        h_ref[0, pl.ds(b * quarter, quarter), :] = norm_rows(
-            x_out[b].astype(F32), norm_ref[0:1, :], norm_ref[1:2, :]
-        ).astype(BF16)
-    swap = remote(h_ref.at[0], h_ref.at[1], send_h, got_h, here.partner)
-    swap.start()
-    block.relay(0)
-    block.relay(1)
-    block.finish()
-    cell.finish()
-    swap.wait()
-
-
 ANY = pl.BlockSpec(memory_space=pl.ANY)
 VMEM = pl.BlockSpec(memory_space=pltpu.VMEM)
 
 
-def gather_first(inputs, shard, norms, collective):
+def rows_at(start, size):
+    return pl.ds(start * size, size)
+
+
+def exact_gelu_both(u):
+    below = 0.5 * (1.0 + lax.erf(u * (0.5**0.5)))
+    density = jnp.exp(-0.5 * u * u) * ((2.0 * jnp.pi) ** -0.5)
+    return u * below, below + u * density
+
+
+class Stores:
+    def __init__(self, sems):
+        self.sems, self.made = sems, []
+
+    def put(self, src, dst):
+        copy = pltpu.make_async_copy(src, dst, self.sems.at[len(self.made)])
+        copy.start()
+        self.made.append((src, dst))
+
+    def finish(self):
+        for i, (src, dst) in enumerate(self.made):
+            pltpu.make_async_copy(src, dst, self.sems.at[i]).wait()
+
+
+def attend_rows(bias, qkv_ref, ctx_ref, lse_ref, chunk, start, block, heads):
+    width = heads * HEAD_DIM
+    spare = qkv_ref.shape[2] - 3 * width
+    rows = pl.ds(start, block)
+    stats = []
+    for h in range(heads):
+        lo = spare + h * HEAD_DIM
+        q = qkv_ref[chunk, rows, lo : lo + HEAD_DIM] * jnp.asarray(HEAD_DIM**-0.5, BF16)
+        k = qkv_ref[chunk, :, width + lo : width + lo + HEAD_DIM]
+        v = qkv_ref[chunk, :, 2 * width + lo : 2 * width + lo + HEAD_DIM]
+        s = mm_nt(q, k) + bias
+        top = jnp.max(s, axis=-1, keepdims=True)
+        e = jnp.exp(s - top)
+        total = jnp.sum(e, axis=-1, keepdims=True)
+        ctx = mm_nn(e.astype(BF16), v) / total
+        ctx_ref[chunk, rows, h * HEAD_DIM : (h + 1) * HEAD_DIM] = ctx.astype(BF16)
+        stats.append(top + jnp.log(total))
+    stats += [jnp.zeros_like(stats[0])] * (8 - heads)
+    lse_ref[chunk, :, rows] = jnp.concatenate(stats, axis=1).T
+
+
+def forward_kernel(heads, *refs):
+    (x_ref, gy_ref, shard_a, shard_1, shard_2, norm_ref, bias_ref) = refs[:7]
+    (full_a, full_1, full_2, h1_out, qkv_out, ctx_out, lse_out, x_out, x2_out, h2_out, act_out, slope_out, gy_out,
+     grad_out) = refs[7:21]
+    (weight, x_in, gy_in, h1, qkv, ctx, lse, fold_out, fold_in, x2, h2, act, slope, gy, stage) = refs[21:36]
+    sems = refs[36:]
+    (cell_sems, swap_send, swap_got, load_sem, store_sems, stage_sems) = (
+        sems[:4], sems[4], sems[5], sems[6], sems[7], sems[8]
+    )
+    here = Here()
+    half, width = x2.shape
+    seq = 2 * half
+    quarter = half // 2
+    inner = heads * HEAD_DIM
+    greet_cross(here, spread_ends(here)[1], here.partner)
+    per = len(Gather.scratch())
+    block_a, block_1, block_2 = (
+        Gather(here, shard, full, sems[9 + per * i : 9 + per * (i + 1)])
+        for i, (shard, full) in enumerate(((shard_a, full_a), (shard_1, full_1), (shard_2, full_2)))
+    )
+    cell_x = ToCell(here, x_ref, x_in, cell_sems[0], cell_sems[1])
+    cell_g = ToCell(here, gy_ref, gy_in, cell_sems[2], cell_sems[3])
+    stores = Stores(store_sems)
+
+    def swap(n, src, dst):
+        return remote(src, dst, swap_send.at[n], swap_got.at[n], here.partner)
+
+    def load(full):
+        copies = [pltpu.make_async_copy(full.at[b], weight.at[b], load_sem.at[b]) for b in range(2)]
+        for copy in copies:
+            copy.start()
+        for copy in copies:
+            copy.wait()
+
+    own, other = pl.ds(0, half), pl.ds(half, half)
+    block_a.start_z()
+    block_a.spread(0)
+    cell_x.start()
+    block_a.spread(1)
+    block_a.relay(0)
+    block_a.relay(1)
+    cell_x.wait()
+    block_1.start_z()
+
+    step = 128
+    per_quarter = quarter // step
+
+    @pl.loop(0, half // step)
+    def _(i):
+        rows = pl.ds(pl.multiple_of((i % per_quarter) * step, step), step)
+        h1[pl.ds(pl.multiple_of(i * step, step), step), :] = norm_rows(
+            x_in[i // per_quarter, rows, :].astype(F32), norm_ref[0:1, :], norm_ref[1:2, :]
+        ).astype(BF16)
+
+    swap_h1 = swap(0, h1.at[own], h1.at[other])
+    swap_h1.start()
+    stores.put(x_in, x_out)
+    block_a.arrive()
+    load(full_a)
+    swap_h1.wait_recv()
+    stores.put(h1, h1_out)
+
+    first = 4 * inner - qkv.shape[2]
+
+    @pl.loop(0, 2)
+    def _(b):
+        for n in range(0, qkv.shape[2], 512):
+            qkv[b, :, n : n + 512] = mm_nn(h1[...], weight[b, :, first + n : first + n + 512]).astype(BF16)
+
+    stores.put(qkv, qkv_out)
+    bias = bias_ref[...]
+    q_block = 256
+    per_chunk = seq // q_block
+
+    @pl.loop(0, 2 * per_chunk)
+    def _(i):
+        pl.when(i == 2)(lambda: block_1.spread(0))
+        pl.when(i == 6)(lambda: block_1.spread(1))
+        pl.when(i == 6)(lambda: block_2.start_z())
+        pl.when(i == 7)(lambda: block_1.relay(0))
+        attend_rows(
+            bias, qkv, ctx, lse, i // per_chunk, pl.multiple_of((i % per_chunk) * q_block, q_block), q_block, heads
+        )
+
+    stores.put(ctx, ctx_out)
+    stores.put(lse, lse_out)
+
+    def branch_tile(rows, n):
+        cols = pl.ds(pl.multiple_of(n * 256, 256), 256)
+        return mm_nt(ctx[0, rows, :], weight[0, cols, 0:inner]) + mm_nt(ctx[1, rows, :], weight[1, cols, 0:inner]), cols
+
+    @pl.loop(0, width // 256)
+    def _(n):
+        part, cols = branch_tile(other, n)
+        fold_out[:, cols] = part.astype(BF16)
+
+    swap_fold = swap(1, fold_out, fold_in)
+    swap_fold.start()
+
+    @pl.loop(0, width // 256)
+    def _(n):
+        part, cols = branch_tile(own, n)
+        for b in range(2):
+            rows = pl.ds(b * quarter, quarter)
+            x2[rows, cols] = x_in[b, :, cols].astype(F32) + part[b * quarter : (b + 1) * quarter]
+
+    block_1.relay(1)
+    swap_fold.wait_recv()
+
+    @pl.loop(0, half // step)
+    def _(i):
+        rows = pl.ds(pl.multiple_of(i * step, step), step)
+        middle = x2[rows, :] + fold_in[rows, :].astype(F32)
+        x2[rows, :] = middle
+        h2[rows, :] = norm_rows(middle, norm_ref[2:3, :], norm_ref[3:4, :]).astype(BF16)
+
+    swap_h2 = swap(2, h2.at[own], h2.at[other])
+    swap_h2.start()
+    stores.put(x2, x2_out)
+    block_1.arrive()
+    load(full_1)
+    block_2.spread(0)
+    swap_h2.wait_recv()
+    stores.put(h2, h2_out)
+    per_unit = width // 256
+
+    @pl.loop(0, 2 * per_unit)
+    def _(i):
+        pl.when(i == 3)(lambda: block_2.spread(1))
+        pl.when(i == 3)(lambda: cell_g.start())
+        pl.when(i == 6)(lambda: block_2.relay(0))
+        b, cols = i // per_unit, pl.ds(pl.multiple_of((i % per_unit) * 256, 256), 256)
+        value, grad = exact_gelu_both(mm_nn(h2[...], weight[b, :, cols]))
+        act[b, :, cols] = value.astype(BF16)
+        slope[b, :, cols] = grad.astype(BF16)
+
+    stores.put(act, act_out)
+    stores.put(slope, slope_out)
+    block_2.relay(1)
+    cell_g.wait()
+
+    @pl.loop(0, 2)
+    def _(b):
+        gy[pl.ds(pl.multiple_of(b * quarter, quarter), quarter), :] = gy_in[b]
+
+    swap_gy = swap(3, gy.at[own], gy.at[other])
+    swap_gy.start()
+    swap_gy.wait_recv()
+    stores.put(gy, gy_out)
+
+    def stage_copy(i):
+        slot = i % 2
+        return pltpu.make_async_copy(
+            stage.at[slot], grad_out.at[:, pl.ds(pl.multiple_of(i * 256, 256), 256), :], stage_sems.at[slot]
+        )
+
+    @pl.loop(0, width // 256)
+    def _(i):
+        pl.when(i >= 2)(lambda: stage_copy(i - 2).wait())
+        left = gy[:, pl.ds(pl.multiple_of(i * 256, 256), 256)].T
+        for b in range(2):
+            stage[i % 2, b] = mm_nn(left, act[b]).astype(BF16)
+        stage_copy(i).start()
+
+    for i in range(width // 256 - 2, width // 256):
+        stage_copy(i).wait()
+    block_2.arrive()
+    for block in (block_a, block_1, block_2):
+        block.sent()
+    cell_x.finish()
+    cell_g.finish()
+    for n, (src, dst) in enumerate(((h1.at[own], h1.at[other]), (fold_out, fold_in), (h2.at[own], h2.at[other]), (gy.at[own], gy.at[other]))):
+        swap(n, src, dst).wait_send()
+    stores.finish()
+
+
+def forward(inputs, cotangent, shards, norms, bias, heads, collective):
     cells, quarter, width = inputs.shape
-    rows = shard.shape[0]
+    rows, wide = shards[0].shape
+    half, seq, inner = 2 * quarter, 4 * quarter, heads * HEAD_DIM
+    part = (3 * inner + 255) // 256 * 256
     dma = pltpu.SemaphoreType.DMA
+    full = ((2, 8 * rows, wide), BF16)
+    kept = [
+        ((seq, width), BF16), ((2, seq, part), BF16), ((2, seq, inner), BF16), ((2, 8, seq), F32),
+        ((2, quarter, width), BF16), ((half, width), F32), ((seq, width), BF16), ((2, seq, wide), BF16),
+        ((2, seq, wide), BF16), ((seq, width), BF16), ((2, width, wide), BF16),
+    ]
+    buffers = [
+        full, ((2, quarter, width), BF16), ((2, quarter, width), BF16), kept[0], kept[1], kept[2], kept[3],
+        ((half, width), BF16), ((half, width), BF16), kept[5], kept[6], kept[7], kept[8], kept[9],
+        ((2, 2, 256, wide), BF16),
+    ]
     return pl.pallas_call(
-        gather_first_kernel,
-        out_shape=[
-            jax.ShapeDtypeStruct((2, 8 * rows, width), BF16),
-            jax.ShapeDtypeStruct((2, 2 * quarter, width), BF16),
-            jax.ShapeDtypeStruct((2, quarter, width), BF16),
-        ],
-        in_specs=[VMEM, VMEM, VMEM],
-        out_specs=[ANY, VMEM, VMEM],
-        scratch_shapes=[dma((2,)), dma((2,)), dma, dma] + Gather.scratch(),
-        compiler_params=pltpu.CompilerParams(collective_id=collective, has_side_effects=True),
-        name="gather_first",
-    )(inputs, shard, norms)
-
-
-def gather_rest_kernel(gy_ref, shard_one, shard_two, full_one, full_two, gy_out, *sems):
-    here = Here()
-    send_g, got_g = sems[:2]
-    greet_cross(here, spread_ends(here)[1])
-    blocks = [Gather(here, shard_one, full_one, sems[2:10]), Gather(here, shard_two, full_two, sems[10:18])]
-    cell = ToCell(here, gy_ref, gy_out, send_g, got_g)
-    for block in blocks:
-        block.start_z()
-    cell.start()
-    for block in blocks:
-        block.spread(0)
-        block.spread(1)
-        block.relay(0)
-        block.relay(1)
-    for block in blocks:
-        block.finish()
-    cell.wait()
-    cell.finish()
-
-
-def gather_rest(cotangent, shard_one, shard_two, collective):
-    cells, quarter, width = cotangent.shape
-    rows = shard_one.shape[0]
-    dma = pltpu.SemaphoreType.DMA
-    return pl.pallas_call(
-        gather_rest_kernel,
-        out_shape=[jax.ShapeDtypeStruct((2, 8 * rows, width), BF16)] * 2
-        + [jax.ShapeDtypeStruct((2, quarter, width), BF16)],
-        in_specs=[VMEM] * 3,
-        out_specs=[ANY] * 3,
-        scratch_shapes=[dma((2,)), dma((2,))] + Gather.scratch() * 2,
-        compiler_params=pltpu.CompilerParams(collective_id=collective, has_side_effects=True),
-        name="gather_rest",
-    )(cotangent, shard_one, shard_two)
+        functools.partial(forward_kernel, heads),
+        out_shape=[jax.ShapeDtypeStruct(*s) for s in [full] * 3 + kept],
+        in_specs=[VMEM] * 7,
+        out_specs=[ANY] * 14,
+        scratch_shapes=[pltpu.VMEM(*s) for s in buffers]
+        + [dma((2,))] * 4 + [dma((4,)), dma((4,)), dma((2,)), dma((10,)), dma((2,))]
+        + Gather.scratch() * 3,
+        compiler_params=pltpu.CompilerParams(
+            collective_id=collective, has_side_effects=True, vmem_limit_bytes=67043328
+        ),
+        name="forward",
+    )(inputs, cotangent, *shards, norms, bias)
 
 
 class Reduce:
@@ -691,7 +870,36 @@
     return cur
 
 
-def per_device(
+def update(
+    outputs, input_grad, norm_sum, attend_sum, expand_sum, reduce_sum, step_count, norm_params, norm_first, norm_second,
+    attend_weight, attend_first, attend_second, output_weight, output_first, output_second,
+    expand_weight, expand_first, expand_second, reduce_weight, reduce_first, reduce_second,
+):
+    width = attend_weight.shape[2]
+    step_number = step_count[0].astype(F32)
+    norm_new = adam_step(norm_params, norm_first, norm_second, norm_sum, norm_rate, 0.0, step_number)
+    attend_reduced = jnp.stack([attend_sum[:, i * width : (i + 1) * width] for i in range(1, 4)])
+    attend_new = adam_step(
+        attend_weight, attend_first, attend_second, attend_reduced, 2.0 * D ** (-0.5), decay_rate, step_number
+    )
+    output_new = adam_step(
+        output_weight, output_first, output_second, attend_sum[:, :width].T,
+        2.0 * (2 * D // SEQ) ** (-0.5), decay_rate, step_number,
+    )
+    expand_new = adam_step(
+        expand_weight, expand_first, expand_second, expand_sum, 2.0 * D ** (-0.5), decay_rate, step_number
+    )
+    reduce_new = adam_step(
+        reduce_weight, reduce_first, reduce_second, reduce_sum.T, 2.0 * FF ** (-0.5), decay_rate, step_number
+    )
+    return (
+        outputs, input_grad,
+        norm_new[0], norm_new[1], norm_new[2][0:2], norm_new[2][2:4],
+        *attend_new, *output_new, *expand_new, *reduce_new,
+    )
+
+
+def per_device_plain(
     inputs, cotangent, gene_counts, step_count, norm_params, norm_first, norm_second,
     attend_weight, attend_first, attend_second, output_weight, output_first, output_second,
     expand_weight, expand_first, expand_second, reduce_weight, reduce_first, reduce_second,
@@ -718,37 +926,27 @@
 
     def from_cell(rows):
         rows = rows.astype(BF16)
-        if kernels:
-            flip_rows = jnp.concatenate([rows[quarter:], rows[:quarter]], 0)
-            rows = jnp.where(m_low == 1, flip_rows, rows)
         got = [routes.cell(rows[k * quarter : (k + 1) * quarter], k, back=True) for k in range(2)]
         flip = m_low == 1
         return jnp.stack([jnp.where(flip, got[1], got[0]), jnp.where(flip, got[0], got[1])]).astype(F32)
 
     attend_shard = jnp.concatenate(
-        [attend_weight[0], attend_weight[1], attend_weight[2], output_weight.T], axis=1
+        [output_weight.T, attend_weight[0], attend_weight[1], attend_weight[2]], axis=1
     ).astype(BF16)
     expand_shard = expand_weight.astype(BF16)
     reduce_shard = reduce_weight.T.astype(BF16)
 
-    kernels = routes.dp == 8 and routes.mp == 4
-    if kernels:
-        attend_w, h1, x_mine = gather_first(inputs, attend_shard, norm_full[0:2], 1)
-        x_mine = x_mine.reshape(half, -1).astype(F32)
-        expand_w, reduce_w, gy_mine = gather_rest(cotangent, expand_shard, reduce_shard, 2)
-        gy_mine = gy_mine.reshape(half, -1)
-    else:
-        x_mine = to_cell(inputs).astype(F32)
-        attend_w = [assemble(pieces, mask) for pieces in gather_shards(routes, attend_shard)]
-        expand_w = [assemble(pieces, mask) for pieces in gather_shards(routes, expand_shard)]
-        reduce_w = [assemble(pieces, mask) for pieces in gather_shards(routes, reduce_shard)]
-        gy_mine = to_cell(cotangent)
+    x_mine = to_cell(inputs).astype(F32)
+    attend_w = [assemble(pieces, mask) for pieces in gather_shards(routes, attend_shard)]
+    expand_w = [assemble(pieces, mask) for pieces in gather_shards(routes, expand_shard)]
+    reduce_w = [assemble(pieces, mask) for pieces in gather_shards(routes, reduce_shard)]
+    gy_mine = to_cell(cotangent)
 
     other_counts = routes.partner(gene_counts)
     mine = jnp.where(m_high == c, gene_counts, other_counts)
     count = jnp.where(m_low == 1, mine[1], mine[0])
     inside = jnp.arange(quarter)
-    first = 0 if kernels else m_low
+    first = m_low
     positions = jnp.concatenate(
         [h * half + b * quarter + inside for h, b in ((c, first), (c, 1 - first), (1 - c, first), (1 - c, 1 - first))]
     )
@@ -761,10 +959,10 @@
         return partial[:half] + routes.partner(partial[half:].astype(BF16)).astype(F32)
 
     normed, scaled_one, inv_one = normalize(x_mine, norm_full[0], norm_full[1])
-    h1 = h1.reshape(seq, -1) if kernels else both(normed.astype(BF16))
-    qkv = jnp.stack([mm_nn(h1, w[:, : 3 * width]).astype(BF16) for w in attend_w])
+    h1 = both(normed.astype(BF16))
+    qkv = jnp.stack([mm_nn(h1, w[:, width:]).astype(BF16) for w in attend_w])
     ctx, lse = attend(qkv, bias[None, :], heads)
-    branch = mm_nt(ctx[0], attend_w[0][:, 3 * width :]) + mm_nt(ctx[1], attend_w[1][:, 3 * width :])
+    branch = mm_nt(ctx[0], attend_w[0][:, :width]) + mm_nt(ctx[1], attend_w[1][:, :width])
     x2 = x_mine + fold(branch)
     normed, scaled_two, inv_two = normalize(x2, norm_full[2], norm_full[3])
     h2 = both(normed.astype(BF16))
@@ -783,53 +981,112 @@
     grad_in, gain_two, shift_two = normalize_back(gh2, scaled_two, inv_two, norm_full[2])
     gx2 = gy_mine.astype(F32) + grad_in
     gb = both(gx2.astype(BF16))
-    grad_ctx = jnp.stack([mm_nn(gb, w[:, 3 * width :]).astype(BF16) for w in attend_w])
+    grad_ctx = jnp.stack([mm_nn(gb, w[:, :width]).astype(BF16) for w in attend_w])
     gq, gkv = attend_back(qkv, grad_ctx, ctx, lse, bias[:, None], heads)
     attend_grad = [
         jnp.concatenate(
-            [mm_tn(h1, gq[i]), mm_tn(h1, gkv[i]), mm_tn(gb, ctx[i])], axis=1
+            [mm_tn(gb, ctx[i]), mm_tn(h1, gq[i]), mm_tn(h1, gkv[i])], axis=1
         ).astype(BF16)
         for i in range(2)
     ]
     gh1 = fold(
         sum(
-            mm_nt(gq[i], attend_w[i][:, :width]) + mm_nt(gkv[i], attend_w[i][:, width : 3 * width])
+            mm_nt(gq[i], attend_w[i][:, width : 2 * width]) + mm_nt(gkv[i], attend_w[i][:, 2 * width :])
             for i in range(2)
         )
     )
     grad_in, gain_one, shift_one = normalize_back(gh1, scaled_one, inv_one, norm_full[0])
     input_grad = from_cell(gx2 + grad_in)
 
-    if kernels:
-        reduce_sum = reduce_block(jnp.stack(reduce_grad), 3)
-        expand_sum = reduce_block(jnp.stack(expand_grad), 3)
-        attend_sum = reduce_block(jnp.stack(attend_grad), 3)
-    else:
-        reduce_sum = scatter_grads(routes, reduce_grad, mask)
-        expand_sum = scatter_grads(routes, expand_grad, mask)
-        attend_sum = scatter_grads(routes, attend_grad, mask)
+    reduce_sum = scatter_grads(routes, reduce_grad, mask)
+    expand_sum = scatter_grads(routes, expand_grad, mask)
+    attend_sum = scatter_grads(routes, attend_grad, mask)
     norm_sum = scatter_norms(routes, jnp.stack([gain_one, shift_one, gain_two, shift_two]), d, m)
 
-    step_number = step_count[0].astype(F32)
-    norm_new = adam_step(norm_params, norm_first, norm_second, norm_sum, norm_rate, 0.0, step_number)
-    attend_reduced = jnp.stack([attend_sum[:, i * width : (i + 1) * width] for i in range(3)])
-    attend_new = adam_step(
-        attend_weight, attend_first, attend_second, attend_reduced, 2.0 * D ** (-0.5), decay_rate, step_number
-    )
-    output_new = adam_step(
-        output_weight, output_first, output_second, attend_sum[:, 3 * width :].T,
-        2.0 * (2 * D // SEQ) ** (-0.5), decay_rate, step_number,
-    )
-    expand_new = adam_step(
-        expand_weight, expand_first, expand_second, expand_sum, 2.0 * D ** (-0.5), decay_rate, step_number
-    )
-    reduce_new = adam_step(
-        reduce_weight, reduce_first, reduce_second, reduce_sum.T, 2.0 * FF ** (-0.5), decay_rate, step_number
-    )
-    return (
-        outputs, input_grad,
-        norm_new[0], norm_new[1], norm_new[2][0:2], norm_new[2][2:4],
-        *attend_new, *output_new, *expand_new, *reduce_new,
+    return update(
+        outputs, input_grad, norm_sum, attend_sum, expand_sum, reduce_sum, step_count, norm_params, norm_first,
+        norm_second, attend_weight, attend_first, attend_second, output_weight, output_first, output_second,
+        expand_weight, expand_first, expand_second, reduce_weight, reduce_first, reduce_second,
+    )
+
+
+def per_device(
+    inputs, cotangent, gene_counts, step_count, norm_params, norm_first, norm_second,
+    attend_weight, attend_first, attend_second, output_weight, output_first, output_second,
+    expand_weight, expand_first, expand_second, reduce_weight, reduce_first, reduce_second,
+):
+    routes = Routes(lax.axis_size("dp"), lax.axis_size("mp"))
+    d, m = lax.axis_index("dp"), lax.axis_index("mp")
+    c = d % 2
+    cells, quarter, _ = inputs.shape
+    assert routes.mp == 4 and 2 * cells == routes.mp and routes.dp == 8
+    half = 2 * quarter
+    seq = 2 * half
+    heads = attend_weight.shape[2] // HEAD_DIM
+    width = heads * HEAD_DIM
+    m_low, m_high = m % 2, m // 2
+
+    norm_full = gather_norms(routes, norm_params, d, m)
+    shards = (
+        jnp.concatenate([output_weight.T, attend_weight[0], attend_weight[1], attend_weight[2]], axis=1).astype(BF16),
+        expand_weight.astype(BF16),
+        reduce_weight.T.astype(BF16),
+    )
+    other_counts = routes.partner(gene_counts)
+    mine = jnp.where(m_high == c, gene_counts, other_counts)
+    count = jnp.where(m_low == 1, mine[1], mine[0])
+    inside = jnp.arange(half)
+    positions = jnp.concatenate([c * half + inside, (1 - c) * half + inside])
+    bias = jnp.where(positions < 1 + count, 0.0, masked_score).astype(F32)
+
+    (attend_w, expand_w, reduce_w, h1, qkv, ctx, lse, x_mine, x2, h2, act, slope, gy, reduce_grad) = forward(
+        inputs, cotangent, shards, norm_full, bias[None, :], heads, 1
+    )
+
+    def both(rows):
+        return jnp.concatenate([rows, routes.partner(rows)], 0)
+
+    def fold(partial):
+        return partial[:half] + routes.partner(partial[half:].astype(BF16)).astype(F32)
+
+    def from_cell(rows):
+        rows = rows.astype(BF16)
+        flip_rows = jnp.concatenate([rows[quarter:], rows[:quarter]], 0)
+        rows = jnp.where(m_low == 1, flip_rows, rows)
+        got = [routes.cell(rows[k * quarter : (k + 1) * quarter], k, back=True) for k in range(2)]
+        flip = m_low == 1
+        return jnp.stack([jnp.where(flip, got[1], got[0]), jnp.where(flip, got[0], got[1])]).astype(F32)
+
+    _, scaled_one, inv_one = normalize(x_mine.reshape(half, -1).astype(F32), norm_full[0], norm_full[1])
+    _, scaled_two, inv_two = normalize(x2, norm_full[2], norm_full[3])
+    outputs = from_cell(x2 + fold(mm_nt(act[0], reduce_w[0]) + mm_nt(act[1], reduce_w[1])))
+    reduce_sum = reduce_block(reduce_grad, 3)
+    grad_hidden = [(mm_nn(gy, reduce_w[i]) * slope[i].astype(F32)).astype(BF16) for i in range(2)]
+    expand_grad = [mm_tn(h2, g).astype(BF16) for g in grad_hidden]
+    gh2 = fold(mm_nt(grad_hidden[0], expand_w[0]) + mm_nt(grad_hidden[1], expand_w[1]))
+    grad_in, gain_two, shift_two = normalize_back(gh2, scaled_two, inv_two, norm_full[2])
+    gx2 = gy[:half].astype(F32) + grad_in
+    gb = both(gx2.astype(BF16))
+    grad_ctx = jnp.stack([mm_nn(gb, attend_w[i][:, :width]).astype(BF16) for i in range(2)])
+    gq, gkv = attend_back(qkv[:, :, -3 * width :], grad_ctx, ctx, lse.transpose(0, 2, 1), bias[:, None], heads)
+    attend_grad = [
+        jnp.concatenate([mm_tn(gb, ctx[i]), mm_tn(h1, gq[i]), mm_tn(h1, gkv[i])], axis=1).astype(BF16) for i in range(2)
+    ]
+    gh1 = fold(
+        sum(
+            mm_nt(gq[i], attend_w[i][:, width : 2 * width]) + mm_nt(gkv[i], attend_w[i][:, 2 * width :])
+            for i in range(2)
+        )
+    )
+    grad_in, gain_one, shift_one = normalize_back(gh1, scaled_one, inv_one, norm_full[0])
+    input_grad = from_cell(gx2 + grad_in)
+    expand_sum = reduce_block(jnp.stack(expand_grad), 3)
+    attend_sum = reduce_block(jnp.stack(attend_grad), 3)
+    norm_sum = scatter_norms(routes, jnp.stack([gain_one, shift_one, gain_two, shift_two]), d, m)
+    return update(
+        outputs, input_grad, norm_sum, attend_sum, expand_sum, reduce_sum, step_count, norm_params, norm_first,
+        norm_second, attend_weight, attend_first, attend_second, output_weight, output_first, output_second,
+        expand_weight, expand_first, expand_second, reduce_weight, reduce_first, reduce_second,
     )
 
 
@@ -838,7 +1095,7 @@
     attend_spec, col, row = P(None, "dp", "mp"), P("mp", "dp"), P("dp", "mp")
     tokens = P("dp", "mp", None)
     return jax.shard_map(
-        per_device,
+        per_device if mesh.shape["dp"] == 8 else per_device_plain,
         mesh=mesh,
         in_specs=(tokens, tokens, P("dp"), P(), norms, norms, norms)
         + (attend_spec,) * 3 + (col,) * 3 + (row,) * 3 + (col,) * 3,

time: 820 us -> 739 us (0.901)
  matrix products: 136 us -> 77 us
  Pallas kernels: 523 us -> 502 us
    dot_general x28 -> x20, matrix products: 136 us -> 77 us  [mm(): lax.dot_general(left, right, (dims, ((), ())), preferred_element_type=F32)]
    pallas_call x3 -> x1, Pallas kernels: 240 us -> 207 us  [forward(): pl.pallas_call(functools.partial(forward_kernel, heads), out_shape=[jax.S...]
    pallas_call x3, Pallas kernels: 247 us -> 259 us  [reduce_block(): pl.pallas_call(reduce_kernel, out_shape=jax.ShapeDtypeStruct((rows, width...]
    ppermute x22 -> x19, waiting for transfers between devices: 27.9 us -> 25.7 us  [send(): return lax.ppermute(value, AXES, pairs)]
    ppermute x22 -> x19, starting transfers between devices: 31.7 us -> 29.7 us  [send(): return lax.ppermute(value, AXES, pairs)]
  transfers between devices with their start and end apart: 22 -> 19, of which waited for: 8 -> 7; matrix products, arithmetic and copies ran while one was open for 18% -> 14% of each run, Pallas kernels for 52% -> 16%
where the time goes in v3:
time: 739 us; the launch traced here: 725 us
  Pallas kernels  502 us (68%)
  matrix products  77 us (10%)
  other arithmetic  47.2 us (6%)
  local copies, waits for them, and re-layouts  39.3 us (5%)
  starting transfers between devices  29.7 us (4%)
  waiting for transfers between devices  25.7 us (3%)
    pallas_call x3, Pallas kernels, reduce_block(): pl.pallas_call(reduce_kernel, out_shape=jax.ShapeDtypeStruct((rows, width...  259 us
    pallas_call x1, Pallas kernels, forward(): pl.pallas_call(functools.partial(forward_kernel, heads), out_shape=[jax.S...  207 us
    dot_general x20, matrix products, mm(): lax.dot_general(left, right, (dims, ((), ())), preferred_element_type=F32)  77 us
    pallas_call x1, Pallas kernels, attend_back(): pl.pallas_call(functools.partial(attend_back_kernel, heads), grid=(chunks...  35.1 us
    ppermute x19, starting transfers between devices, send(): return lax.ppermute(value, AXES, pairs)  29.7 us
    ppermute x19, waiting for transfers between devices, send(): return lax.ppermute(value, AXES, pairs)  25.7 us
  transfers between devices with their start and end apart: 19, of which 7 were waited for; matrix products, arithmetic and copies ran while one was open for 14% of the time, Pallas kernels for 16%

profile of v3, /device:TPU:1, one launch (start us, length us, event | category | flops | bytes accessed | tf_op | source)
XLA Modules:
  0.0 724.7 jit_solution(8662244829758459965)
XLA Ops:
  21.4 207.3 %forward.1 = (bf16[2,1280,1280]{2,1,0:T(8,128)(2,1)}, bf16[2,1280,1280]{2,1,0:T(8,128)(2,1)}, bf16[2,1280,1280]{2,1,0:T(8,128)(2,1)}, bf16[1024,1280]{1,0:T(8,12...) custom-call(bf16[2,256,1280]{2,1,0:T(8,128)(2,1)} %refs_0_.1, ...), custom_call_target="tpu_custom_call" | custom-call | tf_op jit(solution)/shard_map/forward/pallas_call | solution.py:704
  228.7 8.7 %fusion.2 = bf16[1024,1280]{1,0:T(8,128)(2,1)} fusion(bf16[1024,1280]{1,0:T(8,128)(2,1)} %get-tuple-element.37, bf16[2,1280,1280]{2,1,0:T(8,128)(2,1)} %get-tuple-element.36, bf16[2,1024,1280]{2,1,0:T(8,128)(2,1)} %get-tuple-element.38), kind=kOutput, calls=%fused_computation.7 | convolution fusion | flops 3359375360 | bytes 11141120 | tf_op jit(solution)/shard_map/dot_general | solution.py:33
  237.4 5.2 fusion.3
  242.7 4.4 slice.192.q_ref.kv_ref
  249.0 91.4 %reduce_block.5 = f32[160,1280]{1,0:T(8,128)} custom-call(bf16[2,1280,1280]{2,1,0:T(8,128)(2,1)} %get-tuple-element.49.grads_ref), custom_call_target="tpu_custom_call" | custom-call | tf_op jit(solution)/shard_map/reduce_block/pallas_call | solution.py:834
  341.7 5.7 fusion
  347.5 3.9 fusion.1
  354.7 86.1 %reduce_block.4 = f32[160,1280]{1,0:T(8,128)} custom-call(bf16[2,1280,1280]{2,1,0:T(8,128)(2,1)} %pad_maximum_fusion.1.grads_ref), custom_call_target="tpu_custom_call" | custom-call | tf_op jit(solution)/shard_map/reduce_block/pallas_call | solution.py:834
  440.8 6.5 fusion.5
  447.3 3.6 convolution_add_fusion
  454.5 5.9 fusion.10
  460.4 3.6 convolution_add_fusion.1
  474.6 3.7 multiply_subtract_fusion.1
  481.9 3.9 fusion.79
  487.6 6.5 collective-permute-start.7
  502.3 35.1 %attend_back.1 = (bf16[2,1024,320]{2,1,0:T(8,128)(2,1)}, bf16[2,1024,640]{2,1,0:T(8,128)(2,1)}) custom-call(f32[1024,1]{1,0:T(8,128)} %broadcast_select_fusion.bias_ref, bf16[2,1024,960]{2,1,0:T(8,128)(2,1)} %slice.192.q_ref.kv_ref, bf16[2,1024,320]{2,1,0:T(8,128)(2,1)} %pad_maximum_fusion.3.g_ref, bf16[2,1024,320]{2,1,0:T(8,128)(2,1)} %get-tuple-element.43.o_ref, ...), custom_call_target="tpu_custom_call" | custom-call | flops 26843545600 | bytes 13107200 | tf_op jit(solution)/shard_map/attend_back/pallas_call | solution.py:155
  537.5 4.6 fusion.28
  568.2 5.3 concatenate.131
  573.4 4.4 fusion.27
  577.8 6.4 concatenate.127
  584.2 5.2 pad_maximum_fusion.grads_ref
  589.5 82.0 %reduce_block.3 = f32[160,1280]{1,0:T(8,128)} custom-call(bf16[2,1280,1280]{2,1,0:T(8,128)(2,1)} %pad_maximum_fusion.grads_ref), custom_call_target="tpu_custom_call" | custom-call | tf_op jit(solution)/shard_map/reduce_block/pallas_call | solution.py:834
  697.1 14.6 %collective-permute-done.18 = f32[4,40]{1,0:T(4,128)S(1)} collective-permute-done((f32[4,40]{1,0:T(4,128)S(1)}, f32[4,40]{1,0:T(4,128)S(1)}, u32[]{:S(2)}, u32[]{:S(2)}) %collective-permute-start.18) | collective-permute-done | bytes 672 | tf_op jit(solution)/shard_map/ppermute | solution.py:202
  713.0 6.7 collective-permute-done.13
  (245 shorter events, 110.1 us)
Async XLA Ops:
  0.7 8.4 %collective-permute-start.5 = (s32[2]{0:T(128)}, s32[2]{0:T(128)S(1)}, u32[]{:S(2)}, u32[]{:S(2)}) collective-permute-start(s32[2]{0:T(128)} %param.21), channel_id=1, source_target_pairs={{0,4},{1,5},{2,6},{3,7},{4,0},{5,1},{6,2},{7,3},{8,12},{9,13},{10,... | collective-permute-start | bytes 32 | tf_op jit(solution)/shard_map/ppermute | solution.py:202
  0.8 8.3 %collective-permute-start = (f32[4,40]{1,0:T(4,128)}, f32[4,40]{1,0:T(4,128)S(1)}, u32[]{:S(2)}, u32[]{:S(2)}) collective-permute-start(f32[4,40]{1,0:T(4,128)} %param.23), channel_id=1, source_target_pairs={{0,1},{1,0},{2,3},{3,2},{4,5},{5,4},{6,7},{7,6},{8,9},{9,8},{10,11... | collective-permute-start | bytes 1928 | tf_op jit(solution)/shard_map/ppermute | solution.py:202
  9.2 4.2 collective-permute-start.1
  13.5 1.5 collective-permute-start.2
  15.0 2.5 collective-permute-start.3
  17.6 2.5 collective-permute-start.4
  249.0 91.4 %copy-start.28 = (f32[2,8,1024]{2,1,0:T(8,128)S(1)}, f32[2,8,1024]{2,1,0:T(8,128)}, u32[]{:S(2)}) copy-start(f32[2,8,1024]{2,1,0:T(8,128)} %get-tuple-element.44) | copy-start | bytes 196612
  249.0 92.7 %copy-start.39 = (bf16[1024,1280]{1,0:T(8,128)(2,1)S(1)}, bf16[1024,1280]{1,0:T(8,128)(2,1)}, u32[]{:S(2)}) copy-start(bf16[1024,1280]{1,0:T(8,128)(2,1)} %get-tuple-element.48) | copy-start | bytes 7864324
  354.7 92.6 %slice-start.10 = ((s8[6553600]{0:T(1024)(128)(4,1)}), s8[2359296]{0:T(1024)(128)(4,1)S(1)}, s32[]{:S(2)}) async-start(s8[6553600]{0:T(1024)(128)(4,1)} %bitcast.172), calls=%async_computation.10 | async-start | bytes 4718592
  454.5 24.2 %collective-permute-start.9 = (bf16[512,1280]{1,0:T(8,128)(2,1)}, bf16[512,1280]{1,0:T(8,128)(2,1)}, u32[]{:S(2)}, u32[]{:S(2)}) collective-permute-start(bf16[512,1280]{1,0:T(8,128)(2,1)} %slice.375), channel_id=1, source_target_pairs={{0,4},{1,5},{2,6},{3,7},{4,0},{5,1},{6,2},{7,3},{8,12},{9,13},{10,... | collective-permute-start | bytes 3932168 | tf_op jit(solution)/shard_map/ppermute | solution.py:202
  465.3 16.5 %collective-permute-start.6 = (bf16[512,1280]{1,0:T(8,128)(2,1)}, bf16[512,1280]{1,0:T(8,128)(2,1)}, u32[]{:S(2)}, u32[]{:S(2)}) collective-permute-start(bf16[512,1280]{1,0:T(8,128)(2,1)} %slice.376), channel_id=1, source_target_pairs={{0,4},{1,5},{2,6},{3,7},{4,0},{5,1},{6,2},{7,3},{8,12},{9,13},{10,... | collective-permute-start | bytes 3932168 | tf_op jit(solution)/shard_map/ppermute | solution.py:202
  485.9 10.2 %collective-permute-start.10 = (bf16[512,1280]{1,0:T(8,128)(2,1)S(1)}, bf16[512,1280]{1,0:T(8,128)(2,1)S(1)}, u32[]{:S(2)}, u32[]{:S(2)}) collective-permute-start(bf16[512,1280]{1,0:T(8,128)(2,1)S(1)} %get-tuple-element.75), channel_id=1, source_target_pairs={{0,4},{1,5},{2,6},{3,7},{4,0},{5,1},{6,2},{7,3},{8,12},{9,13},{10,... | collective-permute-start | bytes 3932168 | tf_op jit(solution)/shard_map/ppermute | solution.py:202
  487.6 225.4 %collective-permute-start.7 = (bf16[256,1280]{1,0:T(8,128)(2,1)}, bf16[256,1280]{1,0:T(8,128)(2,1)}, u32[]{:S(2)}, u32[]{:S(2)}) collective-permute-start(bf16[256,1280]{1,0:T(8,128)(2,1)} %get-tuple-element.88), channel_id=1, source_target_pairs={{1,0},{0,1},{5,2},{4,3},{3,4},{2,5},{7,6},{6,7},{9,8},{8,9},{13,10... | collective-permute-start | bytes 1966088 | tf_op jit(solution)/shard_map/ppermute | solution.py:202
  494.1 218.9 %collective-permute-start.8 = (bf16[256,1280]{1,0:T(8,128)(2,1)}, bf16[256,1280]{1,0:T(8,128)(2,1)}, u32[]{:S(2)}, u32[]{:S(2)}) collective-permute-start(bf16[256,1280]{1,0:T(8,128)(2,1)} %get-tuple-element.89), channel_id=1, source_target_pairs={{0,0},{1,1},{4,2},{5,3},{2,4},{3,5},{6,6},{7,7},{8,8},{9,9},{12,10... | collective-permute-start | bytes 1966088 | tf_op jit(solution)/shard_map/ppermute | solution.py:202
  563.2 111.5 %collective-permute-start.11 = (bf16[512,1280]{1,0:T(8,128)(2,1)}, bf16[512,1280]{1,0:T(8,128)(2,1)}, u32[]{:S(2)}, u32[]{:S(2)}) collective-permute-start(bf16[512,1280]{1,0:T(8,128)(2,1)} %slice.374), channel_id=1, source_target_pairs={{0,4},{1,5},{2,6},{3,7},{4,0},{5,1},{6,2},{7,3},{8,12},{9,13},{10,... | collective-permute-start | bytes 3932168 | tf_op jit(solution)/shard_map/ppermute | solution.py:202
  589.5 83.6 %copy-start.19 = (f32[3,160,320]{2,1,0:T(8,128)S(1)}, f32[3,160,320]{2,1,0:T(8,128)}, u32[]{:S(2)}) copy-start(f32[3,160,320]{2,1,0:T(8,128)} %param.28) | copy-start | bytes 1843204
  589.5 83.6 %copy-start.20 = (f32[3,160,320]{2,1,0:T(8,128)S(1)}, f32[3,160,320]{2,1,0:T(8,128)}, u32[]{:S(2)}) copy-start(f32[3,160,320]{2,1,0:T(8,128)} %param.27) | copy-start | bytes 1843204
  678.5 3.5 collective-permute-start.14
  682.1 2.5 collective-permute-start.15
  684.8 1.2 collective-permute-start.16
  686.1 7.0 collective-permute-start.17
  689.3 23.8 %collective-permute-start.12 = (bf16[256,1280]{1,0:T(8,128)(2,1)S(1)}, bf16[256,1280]{1,0:T(8,128)(2,1)S(1)}, u32[]{:S(2)}, u32[]{:S(2)}) collective-permute-start(bf16[256,1280]{1,0:T(8,128)(2,1)S(1)} %get-tuple-element.82), channel_id=1, source_target_pairs={{1,0},{0,1},{5,2},{4,3},{3,4},{2,5},{7,6},{6,7},{9,8},{8,9},{13,10... | collective-permute-start | bytes 1966088 | tf_op jit(solution)/shard_map/ppermute | solution.py:202
  691.1 28.6 %collective-permute-start.13 = (bf16[256,1280]{1,0:T(8,128)(2,1)S(1)}, bf16[256,1280]{1,0:T(8,128)(2,1)S(1)}, u32[]{:S(2)}, u32[]{:S(2)}) collective-permute-start(bf16[256,1280]{1,0:T(8,128)(2,1)S(1)} %get-tuple-element.83), channel_id=1, source_target_pairs={{0,0},{1,1},{4,2},{5,3},{2,4},{3,5},{6,6},{7,7},{8,8},{9,9},{12,10... | collective-permute-start | bytes 1966088 | tf_op jit(solution)/shard_map/ppermute | solution.py:202
  693.2 18.5 %collective-permute-start.18 = (f32[4,40]{1,0:T(4,128)S(1)}, f32[4,40]{1,0:T(4,128)S(1)}, u32[]{:S(2)}, u32[]{:S(2)}) collective-permute-start(f32[4,40]{1,0:T(4,128)S(1)} %slice_select_fusion.4), channel_id=1, source_target_pairs={{0,1},{1,0},{2,3},{3,2},{4,5},{5,4},{6,7},{7,6},{8,9},{9,8},{10,11... | collective-permute-start | bytes 1928 | tf_op jit(solution)/shard_map/ppermute | solution.py:202
  (55 other events, 449.6 us)
